TPU v7x, 256 devices: a whole 4x4x8 slice. The times are simulated.
256 devices in a mesh: mode: 8 (over y, core), blk: 32 (over z, x).
Axes of the slice: x: 4, y: 4, z: 8, core: 2. Of those that a mesh axis runs over, the one named last changes fastest.
Arguments:
- divergence: float32 [32, 32, 128, 1024], P('blk', None, 'mode')
- neighbours: int32 [32, 2], P('blk'), may hold values from -1 to 31, as said below
- levels: int32 [32], P('blk'), may hold values from 0 to 2
- sweeps: int32 [3], replicated, may hold values from 1 to 2, as said below
Outputs:
- pressure: float32 [32, 32, 128, 1024], P('blk', None, 'mode')
Inputs may be any that keep to these rules, and one draw needn't show every extreme that they name: `neighbours`: row b holds the slots of the columns west (entry 0) and east (entry 1) of the column in slot b along x, -1 beyond the two ends of the 32 columns. The lists are mutual, every slot is named, and every neighbour's slot lies within 3 of b, exactly 3 away for some. Some level has 2 sweeps.
All inputs are finite; a program needn't handle non-finite values.
Results may differ from a plain program's by a relative error of at most 0.0003.
Values sent between devices are 32-bit elements; how exact they have to be, the bound alone decides.
No kernel may reach another device: no remote copies, remote signals or barrier semaphores. Data moves between devices by JAX's collectives and lax.ppermute only.
A program may use at most 128 MiB of HBM per device.

v0:
```python
import functools
import math

import jax
import jax.numpy as jnp
import numpy as np
from jax import lax
from jax.experimental import pallas as pl
from jax.experimental.pallas import tpu as pltpu
from jax.sharding import PartitionSpec as P

NY = 1024
BX = 32
NZ = 128
CITERS = 8
DAMPING = 0.8
REACH = 3
BLOCKS = 8
ROWS = NZ // BLOCKS
DEVICES = 256
F32 = jnp.float32
BF16 = jnp.bfloat16


def sine_table(extent):
    ordinal = np.arange(1, extent + 1)
    angles = np.pi * np.outer(ordinal, ordinal) / (extent + 1)
    matrix = np.sqrt(2.0 / (extent + 1)) * np.sin(angles)
    return matrix, 4.0 * np.sin(np.pi * ordinal / (2 * (extent + 1))) ** 2


def two_terms(array):
    high = np.asarray(array, np.float32).astype(BF16)
    low = (np.asarray(array, np.float64) - high.astype(np.float64)).astype(BF16)
    return high, low


def fourier_class(length, cosines, sines):
    y = np.arange(length)
    columns = []
    for waves, function in ((cosines, np.cos), (sines, np.sin)):
        for m in waves:
            weight = (1.0 if m in (0, NY // 2) else 2.0) / NY
            columns.append(math.sqrt(weight) * function(2 * np.pi * ((m * y) % NY) / NY))
    waves = np.concatenate((np.array(cosines), np.array(sines)))
    return np.stack(columns, axis=1), 4.0 * np.sin(np.pi * waves / NY) ** 2


SX, LX = sine_table(BX)
SB, LB = sine_table(ROWS)
SZ, LZ = sine_table(NZ)
IX = np.concatenate((np.arange(0, BX, 2), np.arange(1, BX, 2)))
JB = np.concatenate((np.arange(0, ROWS, 2), np.arange(1, ROWS, 2)))
T0, K0 = fourier_class(256, range(0, 513, 4), range(4, 512, 4))
T2, K2 = fourier_class(256, range(2, 512, 4), range(2, 512, 4))
T1, K1 = fourier_class(512, range(1, 512, 2), range(1, 512, 2))
KQ = np.concatenate((K0, K2, K1))


def plane_table(parity):
    ways = SX[IX[16 * parity : 16 * parity + 16], :16]
    return np.einsum("ix,jz->ijxz", ways, SB[JB]).reshape(256, 256)


PLANE = np.stack((plane_table(0), plane_table(1)))
ROW_LAMBDA = (LX[IX][:, None] + LB[JB][None, :]).reshape(512, 1)
ZBASIS = np.einsum("jmz,kz->jmk", SZ.reshape(NZ, BLOCKS, ROWS), SB[JB]).reshape(NZ, NZ)
ZSUM = SZ.sum(axis=0).reshape(NZ, 1)


def link_tables():
    scale = np.zeros((2, 4, 32, 4, 2, 16))
    lam = np.zeros((2, 4, 32, 4, 2, 16))
    for half in range(2):
        for q in range(4):
            for a in range(32):
                lam[half, q, a] = LX[IX[a]] + LB[JB][None, None, :]
                for b in range(8 * half, 8 * half + 8):
                    scale[half, q, a, q, a // 16, b] = SX[0, IX[a]] * SB[0, JB[b]]
    return scale.reshape(256, 128), lam.reshape(256, 128)


LINK_SCALE, LINK_LAMBDA = link_tables()
KQ_OWN = np.repeat(KQ.reshape(4, DEVICES).T, 32, axis=1).reshape(DEVICES, 1, 128)


def halves(value):
    high = value.astype(BF16)
    return high, (value - high.astype(F32)).astype(BF16)


def dot3(a, b, dims=(((1,), (0,)), ((), ()))):
    ah, al = a
    bh, bl = b
    mul = functools.partial(lax.dot_general, dimension_numbers=dims, preferred_element_type=F32)
    return mul(ah, bh) + mul(ah, bl) + mul(al, bh)


NT = (((1,), (1,)), ((), ()))
TN = (((0,), (0,)), ((), ()))


def stiffness_scalar(level):
    return lax.shift_left(jnp.int32(1), 2 * level).astype(F32)


def forward_kernel(
    levels, neighbours, sweeps, xa, xb, plane_h, plane_l, t0h, t0l, t2h, t2l, t1h, t1l,
    row_lambda, kq, out, w_out, yh, yl, features,
):
    step = pl.program_id(0)
    for k in range(4):
        a, b = xa[k], xb[3 - k]
        rows = pl.ds(pl.multiple_of((4 * step + k) * 16, 16), 16)
        for parity, v in ((0, a + b), (1, a - b)):
            v0, v1, v2, v3 = (v[:, 256 * n : 256 * n + 256] for n in range(4))
            e0, e1 = v0 + v2, v1 + v3
            for n, part in enumerate((e0 + e1, e0 - e1, v0 - v2, v1 - v3)):
                high, low = halves(part)
                yh[parity, rows, 256 * n : 256 * n + 256] = high
                yl[parity, rows, 256 * n : 256 * n + 256] = low

    @pl.when(step == pl.num_programs(0) - 1)
    def _():
        level = levels[0]
        stiffness = stiffness_scalar(level)
        for parity in range(2):
            plane = (plane_h[parity], plane_l[parity])
            z = []
            for n in range(4):
                cut = slice(256 * n, 256 * n + 256)
                z.append(halves(dot3(plane, (yh[parity, :, cut], yl[parity, :, cut]))))
            odd = tuple(jnp.concatenate((z[2][h], z[3][h]), axis=1) for h in range(2))
            base = stiffness * row_lambda[256 * parity : 256 * parity + 256]
            for q in range(4):
                if q == 0:
                    g = dot3(z[0], (t0h[...], t0l[...]))
                elif q == 1:
                    g = dot3(z[1], (t2h[...], t2l[...]))
                else:
                    cut = slice(256 * (q - 2), 256 * (q - 2) + 256)
                    g = dot3(odd, (t1h[:, cut], t1l[:, cut]))
                w = g / (base + kq[:, 256 * q : 256 * q + 256])
                w_out[256 * parity : 256 * parity + 256, 256 * q : 256 * q + 256] = w
                wb = w.reshape(16, 2, 8, 256)
                place = slice(32 * q + 16 * parity, 32 * q + 16 * parity + 16)
                iota = lax.broadcasted_iota(jnp.int32, (8, 256), 0)
                for half in range(2):
                    first = jnp.zeros((8, 256), F32)
                    for b in range(8):
                        first = jnp.where(iota == b, np.float32(SB[0, JB[8 * half + b]]), first)
                    features[half, place, :] = jnp.sum(wb[:, half] * first[None], axis=1)
                total = np.float32(SX[0, IX[16 * parity]]) * w[:16]
                for a in range(1, 16):
                    total = total + np.float32(SX[0, IX[16 * parity + a]]) * w[16 * a : 16 * a + 16]
                features[2, place, :] = total
        for kind in range(3):
            out[pl.ds(kind, DEVICES, stride=4), :] = features[kind].T
        lane = lax.broadcasted_iota(jnp.int32, (DEVICES, 128), 1)
        meta = jnp.zeros((DEVICES, 128), F32)
        facts = (
            stiffness,
            sweeps[level].astype(F32),
            neighbours[0, 0].astype(F32),
            neighbours[0, 1].astype(F32),
        )
        for n, fact in enumerate(facts):
            meta = jnp.where(lane == n, fact, meta)
        out[pl.ds(3, DEVICES, stride=4), :] = meta


def end_responses(shift, extent):
    half = 0.5 * shift
    ratio = 1.0 / (1.0 + half + jnp.sqrt(half * (half + 2.0)))
    square = ratio * ratio
    power = ratio
    for _ in range(extent.bit_length() - 1):
        power = power * power
    rest = power * power
    below = 1.0 / (1.0 - rest * square)
    return ratio * (1.0 - rest) * below, power * (1.0 - square) * below


def column_kernel(
    own, inbox, k_own, lam_x, lam_z, link_scale, link_lambda, zbasis_h, zbasis_l, zsum,
    out, x_links, t_faces,
):
    del own
    k_row = k_own[0]
    meta = inbox[pl.ds(3, 32, stride=4), :]
    stiff_col = meta[:, 0:1]
    easing_col = 1.0 / stiff_col

    near, far = end_responses(lam_x[...] + k_row * easing_col, ROWS)
    passing, held = [], []
    carry = jnp.zeros((32, 128), F32)
    for m in range(BLOCKS):
        held.append((carry, 1.0 / (1.0 - near * carry)))
        carry = near + far * far * carry * held[-1][1]

    def interfaces(even, odd):
        firsts, offsets = [], []
        offset = jnp.zeros((32, 128), F32)
        for m in range(BLOCKS):
            ratio, scale = held[m]
            first, last = even[m] + odd[m], even[m] - odd[m]
            pushed = (first + near * offset) * scale
            offsets.append(offset)
            firsts.append(pushed)
            offset = last + far * (offset + ratio * pushed)
        above = jnp.zeros((32, 128), F32)
        sides = [None] * BLOCKS
        for m in reversed(range(BLOCKS)):
            ratio, scale = held[m]
            head = firsts[m] + far * scale * above
            below = ratio * head + offsets[m]
            sides[m] = (below + above, below - above)
            above = head
        return sides

    def received(kind, m):
        return inbox[pl.ds(128 * m + kind, 32, stride=4), :]

    even = [received(0, m) for m in range(BLOCKS)]
    odd = [received(1, m) for m in range(BLOCKS)]
    sides = interfaces(even, odd)
    for m in range(BLOCKS):
        x_links[32 * m : 32 * m + 32, 0:128] = sides[m][0]
        x_links[32 * m : 32 * m + 32, 128:256] = sides[m][1]

    links = [
        halves(link_scale[...] / (link_lambda[...] + k_row * np.float32(0.25**level)))
        for level in range(3)
    ]
    stiff_rows = jnp.concatenate([stiff_col] * BLOCKS, axis=0)
    hits = [stiff_rows == np.float32(4.0**level) for level in range(3)]
    x_all = x_links[...]
    faces = jnp.concatenate([received(2, m) for m in range(BLOCKS)], axis=0)
    for level in range(3):
        faces = faces + dot3(halves(jnp.where(hits[level], x_all, 0.0)), links[level])

    turned = faces.T
    for m in range(BLOCKS):
        for parity in range(2):
            t_faces[16 * m : 16 * m + 16, 128 * parity : 128 * parity + 128] = jnp.concatenate(
                [
                    turned[32 * q + 16 * parity : 32 * q + 16 * parity + 16, 32 * m : 32 * m + 32]
                    for q in range(4)
                ],
                axis=1,
            )
    zbasis = (zbasis_h[...], zbasis_l[...])
    modes = dot3(zbasis, halves(t_faces[...]))
    west_end = modes[:, :128] + modes[:, 128:]
    east_end = modes[:, :128] - modes[:, 128:]

    meta_t = meta.T
    facts = jnp.concatenate([meta_t[0:8]] * 4, axis=1)
    stiff, allowed = facts[0:1], facts[1:2]
    west_slot, east_slot = facts[2:3], facts[3:4]
    lane = lax.broadcasted_iota(jnp.int32, (1, 128), 1)
    column = (lane % 32).astype(F32)
    offsets = [o for o in range(-REACH, REACH + 1) if o != 0]
    west_hits = [
        ((west_slot >= 0.0) & (column - west_slot == np.float32(o))).astype(F32) for o in offsets
    ]
    east_hits = [
        ((east_slot >= 0.0) & (column - east_slot == np.float32(o))).astype(F32) for o in offsets
    ]

    def shifted(value, hits_by_offset):
        parts = [
            pltpu.roll(value, o % 128, 1) * hit for o, hit in zip(offsets, hits_by_offset)
        ]
        return ((parts[0] + parts[1]) + (parts[2] + parts[3])) + (parts[4] + parts[5])

    def exchange(first, last):
        return shifted(last, west_hits), shifted(first, east_hits)

    face_near, face_far = end_responses(lam_z[...] + k_row / stiff, BX)
    twice = (allowed > 1.0).astype(F32)
    west1, east1 = exchange(west_end, east_end)
    west1, east1 = west1 * twice, east1 * twice
    first = west_end + face_near * west1 + face_far * east1
    last = east_end + face_far * west1 + face_near * east1
    west2, east2 = exchange(first, last)
    moved = (west2 - west1) + (east2 - east1)
    coarse = stiff * jnp.sum(moved * zsum[...], axis=0, keepdims=True)
    diagonal = stiff * np.float32(2 * NZ + 2 * BX) + np.float32(BX * NZ) * k_row
    target = jnp.broadcast_to(coarse / diagonal, (8, 128))
    coupling = stiff * np.float32(NZ) / diagonal
    both_hits = [coupling * (w + e) for w, e in zip(west_hits, east_hits)]
    correction = DAMPING * target
    for _ in range(CITERS - 1):
        beside = shifted(correction, both_hits)
        correction = correction + DAMPING * (target - correction + beside)
    correction = correction[0:1]
    west3 = west2 + zsum[...] * shifted(correction, west_hits)
    east3 = east2 + zsum[...] * shifted(correction, east_hits)
    first = west_end + face_near * west3 + face_far * east3
    last = east_end + face_far * west3 + face_near * east3
    west4, east4 = exchange(first, last)
    again = twice > 0.0
    west = jnp.where(again, west4, west3)
    east = jnp.where(again, east4, east3)
    sums = jnp.concatenate((west + east, west - east), axis=1)
    t_faces[...] = dot3(zbasis, halves(sums), TN)

    turned = jnp.concatenate(
        [
            jnp.concatenate(
                [
                    t_faces[16 * m : 16 * m + 16, 128 * parity + 32 * q : 128 * parity + 32 * q + 32]
                    for q in range(4)
                    for parity in range(2)
                ],
                axis=0,
            )
            for m in range(BLOCKS)
        ],
        axis=1,
    )
    faces = turned.T
    for m in range(BLOCKS):
        out[pl.ds(128 * m + 2, 32, stride=4), :] = faces[32 * m : 32 * m + 32]
    driven = jnp.zeros((256, 256), F32)
    for level in range(3):
        driven = driven + dot3(halves(jnp.where(hits[level], faces, 0.0)), links[level], NT)
    sides = interfaces(
        [even[m] + driven[32 * m : 32 * m + 32, 0:128] for m in range(BLOCKS)],
        [odd[m] + driven[32 * m : 32 * m + 32, 128:256] for m in range(BLOCKS)],
    )
    for m in range(BLOCKS):
        for kind in range(2):
            out[pl.ds(128 * m + kind, 32, stride=4), :] = sides[m][kind]
        out[pl.ds(128 * m + 3, 32, stride=4), :] = jnp.zeros((32, 128), F32)


def backward_kernel(
    levels, inbox, w_in, plane_h, plane_l, t0h, t0l, t2h, t2l, t1h, t1l, row_lambda, kq,
    out, features, rh, rl,
):
    easing = 1.0 / stiffness_scalar(levels[0])
    for kind in range(3):
        features[kind] = inbox[pl.ds(kind, DEVICES, stride=4), :].T
    iota = lax.broadcasted_iota(jnp.int32, (8, 256), 0)
    firsts = []
    for half in range(2):
        first = jnp.zeros((8, 256), F32)
        for b in range(8):
            first = jnp.where(iota == b, np.float32(SB[0, JB[8 * half + b]]), first)
        firsts.append(first)
    for parity in range(2):
        rows = slice(256 * parity, 256 * parity + 256)
        parts = []
        for q in range(4):
            cut = slice(256 * q, 256 * q + 256)
            place = slice(32 * q + 16 * parity, 32 * q + 16 * parity + 16)
            response = 1.0 / (row_lambda[rows] + kq[:, cut] * easing)
            ends = [features[half, place, :] for half in range(2)]
            side = features[2, place, :]
            pieces = []
            for a in range(16):
                face = np.float32(SX[0, IX[16 * parity + a]]) * side
                for half in range(2):
                    pieces.append(
                        firsts[half] * ends[half][a : a + 1] + face[8 * half : 8 * half + 8]
                    )
            u = w_in[rows, cut] + response * jnp.concatenate(pieces, axis=0)
            parts.append(halves(u))
        odd = tuple(jnp.concatenate((parts[2][h], parts[3][h]), axis=1) for h in range(2))
        ee = dot3(parts[0], (t0h[...], t0l[...]), NT)
        eo = dot3(parts[1], (t2h[...], t2l[...]), NT)
        o = dot3(odd, (t1h[...], t1l[...]), NT)
        total, difference = ee + eo, ee - eo
        o0, o1 = o[:, :256], o[:, 256:]
        for n, part in enumerate((total + o0, difference + o1, total - o0, difference - o1)):
            high, low = halves(part)
            rh[parity, :, 256 * n : 256 * n + 256] = high
            rl[parity, :, 256 * n : 256 * n + 256] = low
    for n in range(4):
        cut = slice(256 * n, 256 * n + 256)
        sides = [
            dot3((plane_h[parity], plane_l[parity]), (rh[parity, :, cut], rl[parity, :, cut]), TN)
            for parity in range(2)
        ]
        plus, minus = sides[0] + sides[1], sides[0] - sides[1]
        for k in range(16):
            out[k, :, cut] = plus[16 * k : 16 * k + 16]
            out[31 - k, :, cut] = minus[16 * k : 16 * k + 16]


def whole(shape):
    return pl.BlockSpec(shape, lambda *_: (0,) * len(shape))


SMEM = pl.BlockSpec(memory_space=pltpu.SMEM)
VMEM = pl.BlockSpec(memory_space=pltpu.VMEM)


def constants():
    tables = []
    for table in (PLANE, T0, T2, T1):
        tables.extend(jnp.asarray(t) for t in two_terms(table))
    tables.append(jnp.asarray(ROW_LAMBDA, F32))
    tables.append(jnp.asarray(KQ[None, :], F32))
    return tables


def run_forward(levels, neighbours, sweeps, x, tables, **kw):
    return pl.pallas_call(
        forward_kernel,
        grid=(4,),
        in_specs=[
            SMEM, SMEM, SMEM,
            pl.BlockSpec((4, 16, NY), lambda i: (i, 0, 0)),
            pl.BlockSpec((4, 16, NY), lambda i: (7 - i, 0, 0)),
        ]
        + [whole(t.shape) for t in tables],
        out_specs=[whole((1024, 128)), whole((512, NY))],
        out_shape=[
            jax.ShapeDtypeStruct((1024, 128), F32),
            jax.ShapeDtypeStruct((512, NY), F32),
        ],
        scratch_shapes=[
            pltpu.VMEM((2, 256, NY), BF16),
            pltpu.VMEM((2, 256, NY), BF16),
            pltpu.VMEM((3, 128, 256), F32),
        ],
        name="forward",
        **kw,
    )(levels, neighbours, sweeps, x, x, *tables)


def run_columns(device, inbox, **kw):
    lam_x = jnp.asarray(np.tile(LX[IX], 4)[None, :], F32)
    lam_z = jnp.asarray(LZ[:, None], F32)
    zbasis = [jnp.asarray(t) for t in two_terms(ZBASIS)]
    tables = [
        lam_x, lam_z, jnp.asarray(LINK_SCALE, F32), jnp.asarray(LINK_LAMBDA, F32), *zbasis,
        jnp.asarray(ZSUM, F32),
    ]
    return pl.pallas_call(
        column_kernel,
        grid_spec=pltpu.PrefetchScalarGridSpec(
            num_scalar_prefetch=1,
            grid=(1,),
            in_specs=[
                whole((1024, 128)),
                pl.BlockSpec((1, 1, 128), lambda i, own: (own[0], 0, 0)),
            ]
            + [whole(t.shape) for t in tables],
            out_specs=whole((1024, 128)),
            scratch_shapes=[pltpu.VMEM((256, 256), F32), pltpu.VMEM((128, 256), F32)],
        ),
        out_shape=jax.ShapeDtypeStruct((1024, 128), F32),
        name="columns",
        **kw,
    )(device, inbox, jnp.asarray(KQ_OWN, F32), *tables)


def run_backward(levels, inbox, w, tables, **kw):
    return pl.pallas_call(
        backward_kernel,
        in_specs=[SMEM] + [VMEM] * (2 + len(tables)),
        out_specs=VMEM,
        out_shape=jax.ShapeDtypeStruct((BX, ROWS, NY), F32),
        scratch_shapes=[
            pltpu.VMEM((3, 128, 256), F32),
            pltpu.VMEM((2, 256, NY), BF16),
            pltpu.VMEM((2, 256, NY), BF16),
        ],
        name="backward",
        **kw,
    )(levels, inbox, w, *tables)


def traded(outbox):
    pieces = outbox.reshape(DEVICES, 4, 128)
    pieces = lax.all_to_all(pieces, ("mode", "blk"), split_axis=0, concat_axis=0, tiled=True)
    return pieces.reshape(4 * DEVICES, 128)


def body(divergence, neighbours, levels, sweeps):
    tables = constants()
    device = lax.axis_index("mode") * 32 + lax.axis_index("blk")
    outbox, w = run_forward(levels, neighbours, sweeps, divergence[0], tables)
    outbox = run_columns(device.astype(jnp.int32)[None], traded(outbox))
    return run_backward(levels, traded(outbox), w, tables)[None]


def solution(mesh):
    return jax.shard_map(
        body,
        mesh=mesh,
        in_specs=(P("blk", None, "mode", None), P("blk", None), P("blk"), P()),
        out_specs=P("blk", None, "mode", None),
        check_vma=False,
    )
```

profile of v0, /device:TPU:1, one launch (start us, length us, event | category | flops | bytes accessed | tf_op | source)
XLA Modules:
  0.0 84.7 jit_solution(17843950551859008936)
XLA Ops:
  0.7 7.4 %forward.1 = (f32[1024,128]{1,0:T(8,128)}, f32[512,1024]{1,0:T(8,128)}) custom-call(s32[1]{0:T(128)S(6)} %copy.23.levels, s32[1,2]{1,0:T(1,128)} %neighbours.1, s32[3]{0:T(128)} %sweeps.1, f32[32,16,1024]{2,1,0:T(8,128)} %bitcast.7, f32[32,16,1024]{2,1,0:T(8,128)} %bitcast.8, bf16[2,256,256]{2,1,0:T(8,128)(2,1)} %constant.47.clone.plane_h, ...), custom_call_target="tpu_custom_call" | custom-call | tf_op jit(solution)/shard_map/forward/pallas_call | solution.py:411
  8.1 15.6 %all-to-all-start = ((f32[256,4,128]{2,1,0:T(4,128)}), f32[256,4,128]{2,1,0:T(4,128)S(1)}, u32[]{:S(2)}, u32[]{:S(2)}) async-start(f32[256,4,128]{2,1,0:T(4,128)} %bitcast.12), calls=%async_computation | async-start | bytes 1048576 | tf_op jit(solution)/shard_map/all_to_all | solution.py:480
  23.8 20.0 %all-to-all-done = f32[256,4,128]{2,1,0:T(4,128)S(1)} async-done(((f32[256,4,128]{2,1,0:T(4,128)}), f32[256,4,128]{2,1,0:T(4,128)S(1)}, u32[]{:S(2)}, u32[]{:S(2)}) %all-to-all-start) | async-done | bytes 524320 | tf_op jit(solution)/shard_map/all_to_all | solution.py:480
  43.8 0.0 copy-start
  43.8 0.8 copy-done
  44.6 6.0 %columns.1 = f32[1024,128]{1,0:T(8,128)} custom-call(s32[1]{0:T(128)} %bitcast.own, f32[1024,128]{1,0:T(8,128)} %bitcast.10, f32[256,1,128]{2,1,0:T(1,128)} %constant.64.clone.k_own, f32[1,128]{1,0:T(1,128)} %constant.57.clone.lam_x, f32[128,1]{1,0:T(8,128)} %constant.58.clone.lam_z, f32[256,128]{1,0:T(8,128)} %constant.61.clone.link_scale, ...), custom_call_target="tpu_custom_call" | custom-call | tf_op jit(solution)/shard_map/columns/pallas_call | solution.py:443
  50.6 27.8 %all_to_all.10 = f32[256,4,128]{2,1,0:T(4,128)} all-to-all(f32[256,4,128]{2,1,0:T(4,128)} %bitcast.11), channel_id=1, replica_groups=mesh['mode'=8,'blk'=32] {'mode','blk'}, dimensions={0} | all-to-all | bytes 1048576 | tf_op jit(solution)/shard_map/all_to_all | solution.py:480
  78.3 6.4 %backward.1 = f32[32,16,1024]{2,1,0:T(8,128)} custom-call(s32[1]{0:T(128)S(6)} %copy.23.levels, f32[1024,128]{1,0:T(8,128)} %bitcast.9, f32[512,1024]{1,0:T(8,128)} %get-tuple-element.8.w_in, bf16[2,256,256]{2,1,0:T(8,128)(2,1)} %constant.47.clone.plane_h, bf16[2,256,256]{2,1,0:T(8,128)(2,1)} %constant.48.clone.plane_l, ...), custom_call_target="tpu_custom_call" | custom-call | tf_op jit(solution)/shard_map/backward/pallas_call | solution.py:463
Async XLA Ops:
  8.1 35.7 %all-to-all-start = ((f32[256,4,128]{2,1,0:T(4,128)}), f32[256,4,128]{2,1,0:T(4,128)S(1)}, u32[]{:S(2)}, u32[]{:S(2)}) async-start(f32[256,4,128]{2,1,0:T(4,128)} %bitcast.12), calls=%async_computation | async-start | bytes 1048576 | tf_op jit(solution)/shard_map/all_to_all | solution.py:480
  43.8 0.8 copy-start
where the time goes:
time: 85 us; the launch traced here: 84.7 us
  blocking collectives  27.8 us (33%)
  waiting for transfers between devices  20 us (24%)
  Pallas kernels  19.8 us (23%)
  starting transfers between devices  15.6 us (18%)
    all_to_all x1, blocking collectives, traded(): lax.all_to_all(pieces, ('mode', 'blk'), split_axis=0, concat_axis=0, tile...  27.8 us
    all_to_all x1, waiting for transfers between devices, traded(): lax.all_to_all(pieces, ('mode', 'blk'), split_axis=0, concat_axis=0, tile...  20 us
    all_to_all x1, starting transfers between devices, traded(): lax.all_to_all(pieces, ('mode', 'blk'), split_axis=0, concat_axis=0, tile...  15.6 us
    pallas_call x1, Pallas kernels, run_forward(): pl.pallas_call(forward_kernel, grid=(4,), in_specs=[SMEM, SMEM, SMEM, pl....  7.44 us
    pallas_call x1, Pallas kernels, run_backward(): pl.pallas_call(backward_kernel, in_specs=[SMEM] + [VMEM] * (2 + len(table...  6.36 us
    pallas_call x1, Pallas kernels, run_columns(): pl.pallas_call(column_kernel, grid_spec=pltpu.PrefetchScalarGridSpec(num_...  5.99 us
  transfers between devices with their start and end apart: 1, of which 1 were waited for; matrix products, arithmetic and copies ran while one was open for 0% of the time, Pallas kernels for 0%

commit v1 on v0

v1 whole, which is shorter than its diff:
```python
import functools
import math

import jax
import jax.numpy as jnp
import numpy as np
from jax import lax
from jax.experimental import pallas as pl
from jax.experimental.pallas import tpu as pltpu
from jax.sharding import PartitionSpec as P

NY = 1024
BX = 32
NZ = 128
CITERS = 8
DAMPING = 0.8
REACH = 3
BLOCKS = 8
ROWS = NZ // BLOCKS
DEVICES = 256
F32 = jnp.float32
BF16 = jnp.bfloat16


def sine_table(extent):
    ordinal = np.arange(1, extent + 1)
    angles = np.pi * np.outer(ordinal, ordinal) / (extent + 1)
    matrix = np.sqrt(2.0 / (extent + 1)) * np.sin(angles)
    return matrix, 4.0 * np.sin(np.pi * ordinal / (2 * (extent + 1))) ** 2


def two_terms(array):
    high = np.asarray(array, np.float32).astype(BF16)
    low = (np.asarray(array, np.float64) - high.astype(np.float64)).astype(BF16)
    return high, low


def fourier_class(length, cosines, sines):
    y = np.arange(length)
    columns = []
    for waves, function in ((cosines, np.cos), (sines, np.sin)):
        for m in waves:
            weight = (1.0 if m in (0, NY // 2) else 2.0) / NY
            columns.append(math.sqrt(weight) * function(2 * np.pi * ((m * y) % NY) / NY))
    waves = np.concatenate((np.array(cosines), np.array(sines)))
    return np.stack(columns, axis=1), 4.0 * np.sin(np.pi * waves / NY) ** 2


def odd_class(residue):
    y = np.arange(128)
    columns = []
    waves = []
    for function in (0, 1):
        for m in range(residue, NY, 8):
            angle = 2 * np.pi * ((m * y) % NY) / NY
            if function == 0:
                column = np.concatenate((np.cos(angle), -np.sin(angle)))
            else:
                column = np.concatenate((np.sin(angle), np.cos(angle)))
                column = column if m < NY // 2 else -column
            columns.append(math.sqrt(2.0 / NY) * column)
            waves.append(min(m, NY - m))
    return np.stack(columns, axis=1), 4.0 * np.sin(np.pi * np.array(waves) / NY) ** 2


SX, LX = sine_table(BX)
SB, LB = sine_table(ROWS)
SZ, LZ = sine_table(NZ)
IX = np.concatenate((np.arange(0, BX, 2), np.arange(1, BX, 2)))
JB = np.concatenate((np.arange(0, ROWS, 2), np.arange(1, ROWS, 2)))
T0, K0 = fourier_class(256, range(0, 513, 4), range(4, 512, 4))
T2, K2 = fourier_class(256, range(2, 512, 4), range(2, 512, 4))
T1, K1 = odd_class(1)
T5, K5 = odd_class(5)
T = np.stack((T0, T2, T1, T5))
KQ = np.concatenate((K0, K2, K1, K5))
ROOT_HALF = math.sqrt(0.5)


def plane_table(parity):
    ways = SX[IX[16 * parity : 16 * parity + 16], :16]
    return np.einsum("ix,jz->ijxz", ways, SB[JB]).reshape(256, 256)


PLANE = np.stack((plane_table(0), plane_table(1)))
ZBASIS = np.einsum("jmz,kz->jmk", SZ.reshape(NZ, BLOCKS, ROWS), SB[JB]).reshape(NZ, NZ)
ZSUM = SZ.sum(axis=0).reshape(NZ, 1)


def link_tables():
    scale = np.zeros((2, 4, 32, 4, 2, 16))
    lam = np.zeros((2, 4, 32, 4, 2, 16))
    for half in range(2):
        for q in range(4):
            for a in range(32):
                lam[half, q, a] = LX[IX[a]] + LB[JB][None, None, :]
                for b in range(8 * half, 8 * half + 8):
                    scale[half, q, a, q, a // 16, b] = SX[0, IX[a]] * SB[0, JB[b]]
    return scale.reshape(256, 128), lam.reshape(256, 128)


LINK_SCALE, LINK_LAMBDA = link_tables()
KQ_OWN = np.repeat(KQ.reshape(4, DEVICES).T, 32, axis=1).reshape(DEVICES, 1, 128)


def halves(value):
    high = value.astype(BF16)
    return high, (value - high.astype(F32)).astype(BF16)


NN = (((1,), (0,)), ((), ()))
NT = (((1,), (1,)), ((), ()))


def dot3(a, b, dims=NN):
    ah, al = a
    bh, bl = b
    return lax.dot_general(
        jnp.concatenate((ah, al, ah), axis=1),
        jnp.concatenate((bh, bh, bl), axis=dims[0][1][0]),
        dims,
        preferred_element_type=F32,
    )


def inverted(value):
    guess = pl.reciprocal(value, approx=True)
    return guess * (2.0 - value * guess)


def stiffness_scalar(level):
    return lax.shift_left(jnp.int32(1), 2 * level).astype(F32)


def per_mode(values):
    iota = lax.broadcasted_iota(jnp.int32, (8, 256), 0)
    halves_of = []
    for half in range(2):
        column = jnp.zeros((8, 256), F32)
        for b in range(8):
            column = jnp.where(iota == b, np.float32(values[JB[8 * half + b]]), column)
        halves_of.append(column)
    return halves_of


def pieces_of(x, x_buffer, x_sems, step):
    first, second = 4 * step, 28 - 4 * step
    return [
        pltpu.make_async_copy(x.at[pl.ds(at, 4)], x_buffer.at[pl.ds(at, 4)], x_sems.at[n, step])
        for n, at in enumerate((first, second))
    ]


def forward_kernel(
    levels, neighbours, sweeps, mode, x, plane_h, plane_l, th, tl, kq,
    out, w_out, x_buffer, p_h, p_l, t_h, t_l, yh, yl, fh, fl, w_buffer, features,
    x_sems, t_sems, w_sems,
):
    tables = [
        pltpu.make_async_copy(source, place, t_sems.at[n])
        for n, (source, place) in enumerate(
            ((th, t_h), (tl, t_l), (plane_h, p_h), (plane_l, p_l))
        )
    ]
    for copy in pieces_of(x, x_buffer, x_sems, 0) + tables[:2]:
        copy.start()
    for step in range(1, 4):
        for copy in pieces_of(x, x_buffer, x_sems, step):
            copy.start()
    for copy in tables[2:]:
        copy.start()

    def fold(step, k):
        for parity in range(2):
            for k in (k,):
                a, b = x_buffer[4 * step + k], x_buffer[31 - 4 * step - k]
                v = a + b if parity == 0 else a - b
                v0, v1, v2, v3 = (v[:, 256 * n : 256 * n + 256] for n in range(4))
                e0, e1 = v0 + v2, v1 + v3
                f, g = v0 - v2, v1 - v3
                f0, f1 = f[:, :128], f[:, 128:] * ROOT_HALF
                g0, g1 = g[:, :128], g[:, 128:] * ROOT_HALF
                turn0, turn1 = f1 - g1, f1 + g1
                parts = (
                    e0 + e1,
                    e0 - e1,
                    jnp.concatenate((f0 + turn0, g0 + turn1), axis=1),
                    jnp.concatenate((f0 - turn0, g0 - turn1), axis=1),
                )
                rows = slice(128 * step + 64 * parity + 16 * k, 128 * step + 64 * parity + 16 * k + 16)
                for q in range(4):
                    high, low = halves(parts[q])
                    yh[q, rows, :] = high
                    yl[q, rows, :] = low

    def transform(step, q):
        rows = slice(128 * step, 128 * step + 128)
        for q in (q,):
            f = dot3((yh[q, rows, :], yl[q, rows, :]), (t_h[q], t_l[q]))
            for parity in range(2):
                place = slice(256 * parity + 64 * step, 256 * parity + 64 * step + 64)
                high, low = halves(f[64 * parity : 64 * parity + 64])
                fh[q, place, :] = high
                fl[q, place, :] = low

    for step in range(4):
        for copy in pieces_of(x, x_buffer, x_sems, step):
            copy.wait()
        if step == 1:
            for copy in tables[:2]:
                copy.wait()
        if step == 3:
            for copy in tables[2:]:
                copy.wait()
        for k in range(4):
            fold(step, k)
            if step > 0:
                transform(step - 1, k)
    for q in range(4):
        transform(3, q)
    level = levels[0]
    stiffness = stiffness_scalar(level)
    lambdas = [stiffness * column for column in per_mode(LB)]
    firsts = per_mode(SB[0])
    sublane = lax.broadcasted_iota(jnp.int32, (8, 256), 0)
    low_side = {size: sublane % (2 * size) < size for size in (4, 2, 1)}

    def summed(values):
        for size in (4, 2, 1):
            merged = []
            for n in range(size):
                one, other = values[n], values[n + size]
                kept = jnp.where(low_side[size], one, other)
                moved = jnp.where(low_side[size], other, one)
                if size == 4:
                    moved = pltpu.roll(moved, 4, 0)
                else:
                    moved = jnp.where(
                        low_side[size],
                        pltpu.roll(moved, 8 - size, 0),
                        pltpu.roll(moved, size, 0),
                    )
                merged.append(kept + moved)
            values = merged
        return values[0]

    copies = []
    for q in range(4):
        base = [column + kq[:, 256 * q : 256 * q + 256] for column in lambdas]
        for parity in range(2):
            rows = slice(256 * parity, 256 * parity + 256)
            g = dot3((p_h[parity], p_l[parity]), (fh[q, rows, :], fl[q, rows, :]))
            place = 32 * q + 16 * parity
            totals = [None, None]
            for group in range(2):
                ends = [[], []]
                for a in range(8 * group, 8 * group + 8):
                    shift = stiffness * np.float32(LX[IX[16 * parity + a]])
                    face = np.float32(SX[0, IX[16 * parity + a]])
                    for half in range(2):
                        row = 16 * a + 8 * half
                        w = g[row : row + 8] * inverted(base[half] + shift)
                        w_buffer[2 * q + parity, row : row + 8, :] = w
                        ends[half].append(w * firsts[half])
                        part = face * w
                        totals[half] = part if a == 0 else totals[half] + part
                at = place + 8 * group
                for half in range(2):
                    features[half, at : at + 8, :] = summed(ends[half])
            for half in range(2):
                features[2, place + 8 * half : place + 8 * half + 8, :] = totals[half]
        if q % 2 == 1:
            copy = pltpu.make_async_copy(
                w_buffer.at[pl.ds(4 * (q // 2), 4)], w_out.at[pl.ds(4 * (q // 2), 4)],
                w_sems.at[q // 2],
            )
            copy.start()
            copies.append(copy)
    last = mode[0] == BLOCKS - 1
    lane = lax.broadcasted_iota(jnp.int32, (8, 128), 1)
    meta = jnp.zeros((8, 128), F32)
    facts = (
        stiffness,
        sweeps[level].astype(F32),
        neighbours[0, 0].astype(F32),
        neighbours[0, 1].astype(F32),
    )
    for n, fact in enumerate(facts):
        meta = jnp.where(lane == n, fact, meta)
    meta = jnp.concatenate([meta] * (DEVICES // 8), axis=0)
    even, odd = features[0].T, features[1].T
    out[pl.ds(0, DEVICES, stride=3), :] = jnp.where(last, even + odd, even)
    out[pl.ds(1, DEVICES, stride=3), :] = jnp.where(last, meta, odd)
    out[pl.ds(2, DEVICES, stride=3), :] = features[2].T
    for copy in copies:
        copy.wait()


def end_responses(shift, extent):
    half = 0.5 * shift
    ratio = 1.0 / (1.0 + half + jnp.sqrt(half * (half + 2.0)))
    square = ratio * ratio
    power = ratio
    for _ in range(extent.bit_length() - 1):
        power = power * power
    rest = power * power
    below = 1.0 / (1.0 - rest * square)
    return ratio * (1.0 - rest) * below, power * (1.0 - square) * below


def column_kernel(
    own, inbox, k_own, lam_x, lam_z, link_scale, link_lambda, zbasis_h, zbasis_l, zback_h, zback_l,
    zsum,
    out, x_links, t_faces,
):
    del own
    k_row = k_own[0]
    meta = inbox[pl.ds(96 * (BLOCKS - 1) + 1, 32, stride=3), :]
    stiff_col = meta[:, 0:1]
    easing_col = 1.0 / stiff_col

    near, far = end_responses(lam_x[...] + k_row * easing_col, ROWS)
    passing, held = [], []
    carry = jnp.zeros((32, 128), F32)
    for m in range(BLOCKS):
        held.append((carry, 1.0 / (1.0 - near * carry)))
        carry = near + far * far * carry * held[-1][1]

    def interfaces(even, odd):
        firsts, offsets = [], []
        offset = jnp.zeros((32, 128), F32)
        for m in range(BLOCKS):
            ratio, scale = held[m]
            first, last = even[m] + odd[m], even[m] - odd[m]
            pushed = (first + near * offset) * scale
            offsets.append(offset)
            firsts.append(pushed)
            offset = last + far * (offset + ratio * pushed)
        above = jnp.zeros((32, 128), F32)
        sides = [None] * BLOCKS
        for m in reversed(range(BLOCKS)):
            ratio, scale = held[m]
            head = firsts[m] + far * scale * above
            below = ratio * head + offsets[m]
            sides[m] = (below + above, below - above)
            above = head
        return sides

    def received(kind, m):
        return inbox[pl.ds(96 * m + kind, 32, stride=3), :]

    even = [received(0, m) for m in range(BLOCKS)]
    odd = [received(1, m) for m in range(BLOCKS - 1)] + [jnp.zeros((32, 128), F32)]
    sides = interfaces(even, odd)
    for m in range(BLOCKS):
        x_links[32 * m : 32 * m + 32, 0:128] = sides[m][0]
        x_links[32 * m : 32 * m + 32, 128:256] = sides[m][1]

    links = [
        halves(link_scale[...] / (link_lambda[...] + k_row * np.float32(0.25**level)))
        for level in range(3)
    ]
    stiff_rows = jnp.concatenate([stiff_col] * BLOCKS, axis=0)
    hits = [stiff_rows == np.float32(4.0**level) for level in range(3)]
    x_all = x_links[...]
    faces = jnp.concatenate([received(2, m) for m in range(BLOCKS)], axis=0)
    for level in range(3):
        faces = faces + dot3(halves(jnp.where(hits[level], x_all, 0.0)), links[level])

    turned = faces.T
    for m in range(BLOCKS):
        for parity in range(2):
            t_faces[16 * m : 16 * m + 16, 128 * parity : 128 * parity + 128] = jnp.concatenate(
                [
                    turned[32 * q + 16 * parity : 32 * q + 16 * parity + 16, 32 * m : 32 * m + 32]
                    for q in range(4)
                ],
                axis=1,
            )
    zbasis = (zbasis_h[...], zbasis_l[...])
    zbasis_t = (zback_h[...], zback_l[...])
    modes = dot3(zbasis, halves(t_faces[...]))
    west_end = modes[:, :128] + modes[:, 128:]
    east_end = modes[:, :128] - modes[:, 128:]

    meta_t = meta.T
    facts = jnp.concatenate([meta_t[0:8]] * 4, axis=1)
    stiff, allowed = facts[0:1], facts[1:2]
    west_slot, east_slot = facts[2:3], facts[3:4]
    lane = lax.broadcasted_iota(jnp.int32, (1, 128), 1)
    column = (lane % 32).astype(F32)
    offsets = [o for o in range(-REACH, REACH + 1) if o != 0]
    west_hits = [
        ((west_slot >= 0.0) & (column - west_slot == np.float32(o))).astype(F32) for o in offsets
    ]
    east_hits = [
        ((east_slot >= 0.0) & (column - east_slot == np.float32(o))).astype(F32) for o in offsets
    ]

    def shifted(value, hits_by_offset):
        parts = [
            pltpu.roll(value, o % 128, 1) * hit for o, hit in zip(offsets, hits_by_offset)
        ]
        return ((parts[0] + parts[1]) + (parts[2] + parts[3])) + (parts[4] + parts[5])

    def exchange(first, last):
        return shifted(last, west_hits), shifted(first, east_hits)

    face_near, face_far = end_responses(lam_z[...] + k_row / stiff, BX)
    twice = (allowed > 1.0).astype(F32)
    west1, east1 = exchange(west_end, east_end)
    west1, east1 = west1 * twice, east1 * twice
    first = west_end + face_near * west1 + face_far * east1
    last = east_end + face_far * west1 + face_near * east1
    west2, east2 = exchange(first, last)
    moved = (west2 - west1) + (east2 - east1)
    coarse = stiff * jnp.sum(moved * zsum[...], axis=0, keepdims=True)
    diagonal = stiff * np.float32(2 * NZ + 2 * BX) + np.float32(BX * NZ) * k_row
    target = jnp.broadcast_to(coarse / diagonal, (8, 128))
    coupling = stiff * np.float32(NZ) / diagonal
    both_hits = [coupling * (w + e) for w, e in zip(west_hits, east_hits)]
    correction = DAMPING * target
    for _ in range(CITERS - 1):
        beside = shifted(correction, both_hits)
        correction = correction + DAMPING * (target - correction + beside)
    correction = correction[0:1]
    west3 = west2 + zsum[...] * shifted(correction, west_hits)
    east3 = east2 + zsum[...] * shifted(correction, east_hits)
    first = west_end + face_near * west3 + face_far * east3
    last = east_end + face_far * west3 + face_near * east3
    west4, east4 = exchange(first, last)
    again = twice > 0.0
    west = jnp.where(again, west4, west3)
    east = jnp.where(again, east4, east3)
    sums = jnp.concatenate((west + east, west - east), axis=1)
    t_faces[...] = dot3(zbasis_t, halves(sums))

    turned = jnp.concatenate(
        [
            jnp.concatenate(
                [
                    t_faces[16 * m : 16 * m + 16, 128 * parity + 32 * q : 128 * parity + 32 * q + 32]
                    for q in range(4)
                    for parity in range(2)
                ],
                axis=0,
            )
            for m in range(BLOCKS)
        ],
        axis=1,
    )
    faces = turned.T
    for m in range(BLOCKS):
        out[pl.ds(96 * m + 2, 32, stride=3), :] = faces[32 * m : 32 * m + 32]
    driven = jnp.zeros((256, 256), F32)
    for level in range(3):
        driven = driven + dot3(halves(jnp.where(hits[level], faces, 0.0)), links[level], NT)
    sides = interfaces(
        [even[m] + driven[32 * m : 32 * m + 32, 0:128] for m in range(BLOCKS)],
        [odd[m] + driven[32 * m : 32 * m + 32, 128:256] for m in range(BLOCKS)],
    )
    for m in range(BLOCKS):
        for kind in range(2):
            out[pl.ds(96 * m + kind, 32, stride=3), :] = sides[m][kind]


def backward_kernel(
    levels, inbox, w_in, back_h, back_l, th, tl, kq, out, features, sums, rows_out, sems,
):
    easing = 1.0 / stiffness_scalar(levels[0])
    for kind in range(3):
        features[kind] = inbox[pl.ds(kind, DEVICES, stride=3), :].T
    firsts, lambdas = per_mode(SB[0]), per_mode(LB)
    for q in range(4):
        base = [column + kq[:, 256 * q : 256 * q + 256] * easing for column in lambdas]
        for parity in range(2):
            place = 32 * q + 16 * parity
            side = features[2, place : place + 16, :]
            terms = []
            for a in range(16):
                shift = np.float32(LX[IX[16 * parity + a]])
                face = np.float32(SX[0, IX[16 * parity + a]])
                pair = []
                for half in range(2):
                    row = 16 * a + 8 * half
                    end = features[half, place + a : place + a + 1, :]
                    drive = firsts[half] * end + face * side[8 * half : 8 * half + 8]
                    w = w_in[2 * q + parity, row : row + 8, :]
                    pair.append(w + drive * inverted(base[half] + shift))
                terms.append(halves(jnp.concatenate(pair, axis=0)))
            u = [jnp.concatenate([t[h] for t in terms], axis=0) for h in range(2)]
            sums[q, 256 * parity : 256 * parity + 256, :] = dot3(u, (th[q], tl[q]), NT)
    copies = []
    for n in range(4):
        cut = slice(256 * n, 256 * n + 256)
        sides = []
        for parity in range(2):
            terms = []
            for k in range(16):
                rows = slice(256 * parity + 16 * k, 256 * parity + 16 * k + 16)
                p0, p2, p1, p5 = (sums[q, rows, :] for q in range(4))
                e = p0 + p2 if n % 2 == 0 else p0 - p2
                half = slice(128 * (n % 2), 128 * (n % 2) + 128)
                turn = (p1 - p5) * ROOT_HALF
                mixed = turn[:, :128] + turn[:, 128:] if n % 2 == 0 else turn[:, 128:] - turn[:, :128]
                f = jnp.concatenate((p1[:, half] + p5[:, half], mixed), axis=1)
                terms.append(halves(e + f if n < 2 else e - f))
            v = [jnp.concatenate([t[h] for t in terms], axis=0) for h in range(2)]
            sides.append(dot3((back_h[parity], back_l[parity]), v))
        for k in range(16):
            rows = slice(16 * k, 16 * k + 16)
            rows_out[k, :, cut] = sides[0][rows] + sides[1][rows]
            rows_out[31 - k, :, cut] = sides[0][rows] - sides[1][rows]
        copy = pltpu.make_async_copy(
            rows_out.at[:, :, pl.ds(256 * n, 256)], out.at[:, :, pl.ds(256 * n, 256)], sems.at[n]
        )
        copy.start()
        copies.append(copy)
    for copy in copies:
        copy.wait()


def whole(shape):
    return pl.BlockSpec(shape, lambda *_: (0,) * len(shape))


SMEM = pl.BlockSpec(memory_space=pltpu.SMEM)
VMEM = pl.BlockSpec(memory_space=pltpu.VMEM)


HBM = pl.BlockSpec(memory_space=pltpu.HBM)
GRANT = pltpu.CompilerParams(vmem_limit_bytes=20 * 2**20)


def constants(back=False):
    tables = []
    for table in (np.swapaxes(PLANE, 1, 2), T) if back else (PLANE, T):
        tables.extend(jnp.asarray(t) for t in two_terms(table))
    tables.append(jnp.asarray(KQ[None, :], F32))
    return tables


def run_forward(levels, neighbours, sweeps, mode, x, **kw):
    return pl.pallas_call(
        forward_kernel,
        in_specs=[SMEM] * 4 + [HBM] * 5 + [VMEM],
        out_specs=[VMEM, HBM],
        out_shape=[
            jax.ShapeDtypeStruct((768, 128), F32),
            jax.ShapeDtypeStruct((8, 256, 256), F32),
        ],
        scratch_shapes=[
            pltpu.VMEM((BX, ROWS, NY), F32),
            pltpu.VMEM((2, 256, 256), BF16),
            pltpu.VMEM((2, 256, 256), BF16),
            pltpu.VMEM((4, 256, 256), BF16),
            pltpu.VMEM((4, 256, 256), BF16),
            pltpu.VMEM((4, 512, 256), BF16),
            pltpu.VMEM((4, 512, 256), BF16),
            pltpu.VMEM((4, 512, 256), BF16),
            pltpu.VMEM((4, 512, 256), BF16),
            pltpu.VMEM((8, 256, 256), F32),
            pltpu.VMEM((3, 128, 256), F32),
            pltpu.SemaphoreType.DMA((2, 4)),
            pltpu.SemaphoreType.DMA((4,)),
            pltpu.SemaphoreType.DMA((2,)),
        ],
        name="forward",
        **kw,
    )(levels, neighbours, sweeps, mode, x, *constants())


def run_columns(device, inbox, **kw):
    lam_x = jnp.asarray(np.tile(LX[IX], 4)[None, :], F32)
    lam_z = jnp.asarray(LZ[:, None], F32)
    zbasis = [jnp.asarray(t) for table in (ZBASIS, ZBASIS.T) for t in two_terms(table)]
    tables = [
        lam_x, lam_z, jnp.asarray(LINK_SCALE, F32), jnp.asarray(LINK_LAMBDA, F32), *zbasis,
        jnp.asarray(ZSUM, F32),
    ]
    return pl.pallas_call(
        column_kernel,
        grid_spec=pltpu.PrefetchScalarGridSpec(
            num_scalar_prefetch=1,
            grid=(1,),
            in_specs=[
                whole((768, 128)),
                pl.BlockSpec((1, 1, 128), lambda i, own: (own[0], 0, 0)),
            ]
            + [whole(t.shape) for t in tables],
            out_specs=whole((768, 128)),
            scratch_shapes=[pltpu.VMEM((256, 256), F32), pltpu.VMEM((128, 256), F32)],
        ),
        out_shape=jax.ShapeDtypeStruct((768, 128), F32),
        name="columns",
        **kw,
    )(device, inbox, jnp.asarray(KQ_OWN, F32), *tables)


def run_backward(levels, inbox, w, **kw):
    tables = constants(True)
    return pl.pallas_call(
        backward_kernel,
        in_specs=[SMEM] + [VMEM] * (2 + len(tables)),
        out_specs=HBM,
        out_shape=jax.ShapeDtypeStruct((BX, ROWS, NY), F32),
        scratch_shapes=[
            pltpu.VMEM((3, 128, 256), F32),
            pltpu.VMEM((4, 512, 256), F32),
            pltpu.VMEM((BX, ROWS, NY), F32),
            pltpu.SemaphoreType.DMA((4,)),
        ],
        compiler_params=GRANT,
        name="backward",
        **kw,
    )(levels, inbox, w, *tables)


def traded(outbox):
    pieces = outbox.reshape(DEVICES, 1, 384)
    pieces = lax.all_to_all(pieces, ("mode", "blk"), split_axis=0, concat_axis=0, tiled=True)
    return pieces.reshape(3 * DEVICES, 128)


def body(divergence, neighbours, levels, sweeps):
    mode = lax.axis_index("mode").astype(jnp.int32)
    device = mode * 32 + lax.axis_index("blk").astype(jnp.int32)
    outbox, w = run_forward(levels, neighbours, sweeps, mode[None], divergence[0])
    outbox = run_columns(device[None], traded(outbox))
    return run_backward(levels, traded(outbox), w)[None]


def solution(mesh):
    return jax.shard_map(
        body,
        mesh=mesh,
        in_specs=(P("blk", None, "mode", None), P("blk", None), P("blk"), P()),
        out_specs=P("blk", None, "mode", None),
        check_vma=False,
    )
```

time: 85 us -> 74.8 us (0.88)
  Pallas kernels: 19.8 us -> 15.6 us
  blocking collectives: 27.8 us -> 24 us
  waiting for transfers between devices: 20 us -> 16.7 us
  starting transfers between devices: 15.6 us -> 16.5 us
    all_to_all x1, blocking collectives: 27.8 us -> 24 us  [traded(): lax.all_to_all(pieces, ('mode', 'blk'), split_axis=0, concat_axis=0, tile...]
    all_to_all x1, waiting for transfers between devices: 20 us -> 16.7 us  [traded(): lax.all_to_all(pieces, ('mode', 'blk'), split_axis=0, concat_axis=0, tile...]
    pallas_call x1, Pallas kernels: 6.36 us -> 3.32 us  [run_backward(): pl.pallas_call(backward_kernel, in_specs=[SMEM] + [VMEM] * (2 + len(table...]
    all_to_all x1, starting transfers between devices: 15.6 us -> 16.5 us  [traded(): lax.all_to_all(pieces, ('mode', 'blk'), split_axis=0, concat_axis=0, tile...]
where the time goes in v1:
time: 74.8 us; the launch traced here: 74.6 us
  blocking collectives  24 us (32%)
  waiting for transfers between devices  16.7 us (22%)
  starting transfers between devices  16.5 us (22%)
  Pallas kernels  15.6 us (21%)
  local copies, waits for them, and re-layouts  0.98 us (1%)
  between operations  0.75 us (1%)
    all_to_all x1, blocking collectives, traded(): lax.all_to_all(pieces, ('mode', 'blk'), split_axis=0, concat_axis=0, tile...  24 us
    all_to_all x1, waiting for transfers between devices, traded(): lax.all_to_all(pieces, ('mode', 'blk'), split_axis=0, concat_axis=0, tile...  16.7 us
    all_to_all x1, starting transfers between devices, traded(): lax.all_to_all(pieces, ('mode', 'blk'), split_axis=0, concat_axis=0, tile...  16.5 us
    pallas_call x1, Pallas kernels, run_forward(): pl.pallas_call(forward_kernel, in_specs=[SMEM] * 4 + [HBM] * 5 + [VMEM],...  6.8 us
    pallas_call x1, Pallas kernels, run_columns(): pl.pallas_call(column_kernel, grid_spec=pltpu.PrefetchScalarGridSpec(num_...  5.46 us
    pallas_call x1, Pallas kernels, run_backward(): pl.pallas_call(backward_kernel, in_specs=[SMEM] + [VMEM] * (2 + len(table...  3.32 us
  transfers between devices with their start and end apart: 1, of which 1 were waited for; matrix products, arithmetic and copies ran while one was open for 0% of the time, Pallas kernels for 0%

profile of v1, /device:TPU:1, one launch (start us, length us, event | category | flops | bytes accessed | tf_op | source)
XLA Modules:
  0.0 74.6 jit_solution(12379724318494688733)
XLA Ops:
  0.7 0.0 copy-start.2
  0.7 6.8 %forward.1 = (f32[768,128]{1,0:T(8,128)}, f32[8,256,256]{2,1,0:T(8,128)}) custom-call(s32[1]{0:T(128)S(6)} %copy.27.levels, s32[1,2]{1,0:T(1,128)} %neighbours.1, s32[3]{0:T(128)} %sweeps.1, s32[1]{0:T(128)} %bitcast.1.mode, f32[32,16,1024]{2,1,0:T(8,128)} %bitcast.9, bf16[2,256,256]{2,1,0:T(8,128)(2,1)} %constant.45.clone.plane_h, ...), custom_call_target="tpu_custom_call" | custom-call | tf_op jit(solution)/shard_map/forward/pallas_call | solution.py:544
  7.5 0.0 copy-start
  7.5 0.0 copy-start.1
  7.5 0.0 copy-start.3
  7.5 0.0 copy-start.5
  7.5 16.5 %all-to-all-start = ((f32[256,1,384]{2,1,0:T(1,128)}), f32[256,1,384]{2,1,0:T(1,128)}, u32[]{:S(2)}, u32[]{:S(2)}) async-start(f32[256,1,384]{2,1,0:T(1,128)} %bitcast.11), calls=%async_computation | async-start | bytes 786432 | tf_op jit(solution)/shard_map/all_to_all | solution.py:621
  24.1 16.7 %all-to-all-done = f32[256,1,384]{2,1,0:T(1,128)} async-done(((f32[256,1,384]{2,1,0:T(1,128)}), f32[256,1,384]{2,1,0:T(1,128)}, u32[]{:S(2)}, u32[]{:S(2)}) %all-to-all-start) | async-done | bytes 393248 | tf_op jit(solution)/shard_map/all_to_all | solution.py:621
  40.8 5.5 %columns.1 = f32[768,128]{1,0:T(8,128)} custom-call(s32[1]{0:T(128)} %bitcast.own, f32[768,128]{1,0:T(8,128)} %bitcast.4.inbox, f32[256,1,128]{2,1,0:T(1,128)} %constant.59.clone.k_own, f32[1,128]{1,0:T(1,128)} %constant.50.clone.lam_x, f32[128,1]{1,0:T(8,128)} %constant.51.clone.lam_z, f32[256,128]{1,0:T(8,128)} %constant.56.clone.link_scale, ...), custom_call_target="tpu_custom_call" | custom-call | tf_op jit(solution)/shard_map/columns/pallas_call | solution.py:581
  46.3 24.0 %all_to_all.10 = f32[256,1,384]{2,1,0:T(1,128)S(1)} all-to-all(f32[256,1,384]{2,1,0:T(1,128)} %bitcast.10), channel_id=1, replica_groups=mesh['mode'=8,'blk'=32] {'mode','blk'}, dimensions={0} | all-to-all | bytes 786432 | tf_op jit(solution)/shard_map/all_to_all | solution.py:621
  70.3 0.0 copy-done.2
  70.3 0.0 copy-done
  70.3 0.0 copy-done.1
  70.3 0.0 copy-done.3
  70.3 0.0 copy-done.5
  70.3 0.0 copy-start.4
  70.3 0.9 %copy-done.4 = bf16[2,256,256]{2,1,0:T(8,128)(2,1)S(1)} copy-done((bf16[2,256,256]{2,1,0:T(8,128)(2,1)S(1)}, bf16[2,256,256]{2,1,0:T(8,128)(2,1)}, u32[]{:S(2)}) %copy-start.4) | copy-done | bytes 262168
  71.2 3.3 %backward.1 = f32[32,16,1024]{2,1,0:T(8,128)} custom-call(s32[1]{0:T(128)S(6)} %copy.27.levels, f32[768,128]{1,0:T(8,128)S(1)} %bitcast.8, f32[8,256,256]{2,1,0:T(8,128)S(1)} %copy-done, bf16[2,256,256]{2,1,0:T(8,128)(2,1)S(1)} %copy-done.4, bf16[2,256,256]{2,1,0:T(8,128)(2,1)S(1)} %copy-done.3, bf16[4,256,256]{2,1,0:T(8,128)(2,1)S(1)} %copy-done.2, ...), custom_call_target="tpu_custom_call" | custom-call | tf_op jit(solution)/shard_map/backward/pallas_call | solution.py:602
Async XLA Ops:
  0.7 69.6 %copy-start.2 = (bf16[4,256,256]{2,1,0:T(8,128)(2,1)S(1)}, bf16[4,256,256]{2,1,0:T(8,128)(2,1)}, u32[]{:S(2)}) copy-start(bf16[4,256,256]{2,1,0:T(8,128)(2,1)} %constant.47.clone.th) | copy-start | bytes 1572868
  7.5 62.8 %copy-start = (f32[8,256,256]{2,1,0:T(8,128)S(1)}, f32[8,256,256]{2,1,0:T(8,128)}, u32[]{:S(2)}) copy-start(f32[8,256,256]{2,1,0:T(8,128)} %get-tuple-element.8.w_in) | copy-start | bytes 6291460
  7.5 62.8 %copy-start.1 = (bf16[4,256,256]{2,1,0:T(8,128)(2,1)S(1)}, bf16[4,256,256]{2,1,0:T(8,128)(2,1)}, u32[]{:S(2)}) copy-start(bf16[4,256,256]{2,1,0:T(8,128)(2,1)} %constant.48.clone.tl) | copy-start | bytes 1572868
  7.5 62.8 %copy-start.3 = (bf16[2,256,256]{2,1,0:T(8,128)(2,1)S(1)}, bf16[2,256,256]{2,1,0:T(8,128)(2,1)}, u32[]{:S(2)}) copy-start(bf16[2,256,256]{2,1,0:T(8,128)(2,1)} %constant.61.clone.back_l) | copy-start | bytes 786436
  7.5 62.8 %copy-start.5 = (f32[1,1024]{1,0:T(1,128)S(1)}, f32[1,1024]{1,0:T(1,128)}, u32[]{:S(2)}) copy-start(f32[1,1024]{1,0:T(1,128)} %constant.49.clone.kq) | copy-start | bytes 12292
  7.5 33.3 %all-to-all-start = ((f32[256,1,384]{2,1,0:T(1,128)}), f32[256,1,384]{2,1,0:T(1,128)}, u32[]{:S(2)}, u32[]{:S(2)}) async-start(f32[256,1,384]{2,1,0:T(1,128)} %bitcast.11), calls=%async_computation | async-start | bytes 786432 | tf_op jit(solution)/shard_map/all_to_all | solution.py:621
  70.3 1.0 %copy-start.4 = (bf16[2,256,256]{2,1,0:T(8,128)(2,1)S(1)}, bf16[2,256,256]{2,1,0:T(8,128)(2,1)}, u32[]{:S(2)}) copy-start(bf16[2,256,256]{2,1,0:T(8,128)(2,1)} %constant.60.clone.back_h) | copy-start | bytes 786436

commit v2 on v1

--- a/solution.py
+++ b/solution.py
@@ -152,16 +152,20 @@
 
 
 def forward_kernel(
-    levels, neighbours, sweeps, mode, x, plane_h, plane_l, th, tl, kq,
-    out, w_out, x_buffer, p_h, p_l, t_h, t_l, yh, yl, fh, fl, w_buffer, features,
+    levels, neighbours, sweeps, mode, x, tables_in, kq,
+    out, w_out, token, x_buffer, p_h, p_l, t_h, t_l, yh, yl, fh, fl, w_buffer, features,
     x_sems, t_sems, w_sems,
 ):
     tables = [
         pltpu.make_async_copy(source, place, t_sems.at[n])
         for n, (source, place) in enumerate(
-            ((th, t_h), (tl, t_l), (plane_h, p_h), (plane_l, p_l))
+            (
+                (tables_in.at[pl.ds(0, 4)], t_h), (tables_in.at[pl.ds(4, 4)], t_l),
+                (tables_in.at[pl.ds(8, 2)], p_h), (tables_in.at[pl.ds(10, 2)], p_l),
+            )
         )
     ]
+    token[...] = jnp.zeros((8, 128), F32)
     for copy in pieces_of(x, x_buffer, x_sems, 0) + tables[:2]:
         copy.start()
     for step in range(1, 4):
@@ -308,23 +312,98 @@
     return ratio * (1.0 - rest) * below, power * (1.0 - square) * below
 
 
+RATIOS, SCALES, NEAR_FAR, FACE_NEAR, FACE_FAR, Z_SUM = 8, 72, 136, 152, 536, 920
+
+
+def prepare_kernel(
+    own, token, k_own, lam_x, lam_z, link_scale, link_lambda, zbasis, zsum,
+    numbers, terms,
+):
+    del own, token
+    k_row = k_own[0]
+    numbers[0:8] = jnp.broadcast_to(k_row, (8, 128))
+    level = lax.broadcasted_iota(jnp.int32, (8, 128), 0)
+    easing = jnp.where(level == 0, 1.0, jnp.where(level == 1, 0.25, 0.0625))
+    near, far = end_responses(lam_x[...] + k_row * easing, ROWS)
+    numbers[NEAR_FAR : NEAR_FAR + 8] = near
+    numbers[NEAR_FAR + 8 : NEAR_FAR + 16] = far
+    carry = jnp.zeros((8, 128), F32)
+    for m in range(BLOCKS):
+        scale = 1.0 / (1.0 - near * carry)
+        numbers[RATIOS + 8 * m : RATIOS + 8 * m + 8] = carry
+        numbers[SCALES + 8 * m : SCALES + 8 * m + 8] = scale
+        carry = near + far * far * carry * scale
+    for level in range(3):
+        shift = k_row * np.float32(0.25**level)
+        face_near, face_far = end_responses(lam_z[...] + shift, BX)
+        numbers[FACE_NEAR + 128 * level : FACE_NEAR + 128 * level + 128] = face_near
+        numbers[FACE_FAR + 128 * level : FACE_FAR + 128 * level + 128] = face_far
+        high, low = halves(link_scale[...] / (link_lambda[...] + shift))
+        terms[256 * level : 256 * level + 256] = high
+        terms[768 + 256 * level : 768 + 256 * level + 256] = low
+    for n in range(4):
+        terms[1536 + 128 * n : 1536 + 128 * n + 128] = zbasis[n]
+    numbers[Z_SUM : Z_SUM + 128] = jnp.broadcast_to(zsum[...], (128, 128))
+
+
 def column_kernel(
-    own, inbox, k_own, lam_x, lam_z, link_scale, link_lambda, zbasis_h, zbasis_l, zback_h, zback_l,
-    zsum,
-    out, x_links, t_faces,
+    inbox, numbers, terms_in, out, x_links, t_faces, turned, passing,
 ):
-    del own
-    k_row = k_own[0]
+    k_row = numbers[0:1]
+    links = (terms_in[0:768], terms_in[768:1536])
+    zsum = numbers[Z_SUM : Z_SUM + 128]
+    zbasis = [terms_in[1536 + 128 * n : 1536 + 128 * n + 128] for n in range(4)]
     meta = inbox[pl.ds(96 * (BLOCKS - 1) + 1, 32, stride=3), :]
     stiff_col = meta[:, 0:1]
-    easing_col = 1.0 / stiff_col
-
-    near, far = end_responses(lam_x[...] + k_row * easing_col, ROWS)
-    passing, held = [], []
-    carry = jnp.zeros((32, 128), F32)
-    for m in range(BLOCKS):
-        held.append((carry, 1.0 / (1.0 - near * carry)))
-        carry = near + far * far * carry * held[-1][1]
+    flat = stiff_col < 2.0
+    middle = stiff_col < 8.0
+
+    meta_t = meta.T
+    facts = jnp.concatenate([meta_t[0:8]] * 4, axis=1)
+    stiff, allowed = facts[0:1], facts[1:2]
+    west_slot, east_slot = facts[2:3], facts[3:4]
+    lane = lax.broadcasted_iota(jnp.int32, (1, 128), 1)
+    first_lane = (lane - lane % 32).astype(F32)
+    row = lax.broadcasted_iota(jnp.int32, (128, 128), 0).astype(F32)
+    west_pick = ((row == first_lane + west_slot) & (west_slot >= 0.0)).astype(F32)
+    east_pick = ((row == first_lane + east_slot) & (east_slot >= 0.0)).astype(F32)
+    diagonal = stiff * np.float32(2 * NZ + 2 * BX) + np.float32(BX * NZ) * k_row
+    coupling = stiff * np.float32(NZ) / diagonal
+    column = lax.broadcasted_iota(jnp.int32, (128, 128), 1).astype(F32)
+    unit = (row == column).astype(F32)
+    step1 = (1.0 - DAMPING) * unit + DAMPING * coupling * (west_pick + east_pick)
+    step1_terms = halves(step1)
+    step2_terms = halves(dot3(step1_terms, step1_terms))
+    step4 = dot3(step2_terms, step2_terms)
+    run2 = step1 + unit
+    run4 = run2 + dot3(halves(run2), step2_terms)
+    run8 = run4 + dot3(halves(run4), halves(step4))
+    picks = jnp.concatenate((west_pick, east_pick), axis=1).astype(BF16)
+    run_high, run_low = halves(run8)
+    sideways = jnp.dot(
+        jnp.concatenate((run_high, run_low), axis=1),
+        jnp.concatenate((picks, picks), axis=0),
+        preferred_element_type=F32,
+    )
+    passing[0], passing[1] = halves(sideways)
+    west_bits = jnp.concatenate([west_pick.astype(BF16)] * 2, axis=0)
+    east_bits = jnp.concatenate([east_pick.astype(BF16)] * 2, axis=0)
+
+    def exchange(first, last):
+        west = jnp.dot(
+            jnp.concatenate(halves(last), axis=1), west_bits, preferred_element_type=F32
+        )
+        east = jnp.dot(
+            jnp.concatenate(halves(first), axis=1), east_bits, preferred_element_type=F32
+        )
+        return west, east
+
+    def by_level(at):
+        values = numbers[at : at + 8]
+        return jnp.where(flat, values[0:1], jnp.where(middle, values[1:2], values[2:3]))
+
+    near, far = by_level(NEAR_FAR), by_level(NEAR_FAR + 8)
+    held = [(by_level(RATIOS + 8 * m), by_level(SCALES + 8 * m)) for m in range(BLOCKS)]
 
     def interfaces(even, odd):
         firsts, offsets = [], []
@@ -356,57 +435,61 @@
         x_links[32 * m : 32 * m + 32, 0:128] = sides[m][0]
         x_links[32 * m : 32 * m + 32, 128:256] = sides[m][1]
 
-    links = [
-        halves(link_scale[...] / (link_lambda[...] + k_row * np.float32(0.25**level)))
-        for level in range(3)
-    ]
-    stiff_rows = jnp.concatenate([stiff_col] * BLOCKS, axis=0)
-    hits = [stiff_rows == np.float32(4.0**level) for level in range(3)]
-    x_all = x_links[...]
-    faces = jnp.concatenate([received(2, m) for m in range(BLOCKS)], axis=0)
-    for level in range(3):
-        faces = faces + dot3(halves(jnp.where(hits[level], x_all, 0.0)), links[level])
-
-    turned = faces.T
-    for m in range(BLOCKS):
-        for parity in range(2):
-            t_faces[16 * m : 16 * m + 16, 128 * parity : 128 * parity + 128] = jnp.concatenate(
+    stiff_rows = jnp.broadcast_to(jnp.concatenate([stiff_col] * BLOCKS, axis=0), (256, 128))
+    hits = [(stiff_rows == np.float32(4.0**level)).astype(BF16) for level in range(3)]
+
+    def spread(value):
+        wide = value.shape[1] // 128
+        return [
+            jnp.concatenate(
                 [
-                    turned[32 * q + 16 * parity : 32 * q + 16 * parity + 16, 32 * m : 32 * m + 32]
-                    for q in range(4)
+                    term[:, 128 * n : 128 * n + 128] * hits[level]
+                    for level in range(3)
+                    for n in range(wide)
                 ],
                 axis=1,
             )
-    zbasis = (zbasis_h[...], zbasis_l[...])
-    zbasis_t = (zback_h[...], zback_l[...])
-    modes = dot3(zbasis, halves(t_faces[...]))
+            for term in halves(value)
+        ]
+
+    faces = jnp.concatenate([received(2, m) for m in range(BLOCKS)], axis=0)
+    faces = faces + dot3(spread(x_links[...]), links)
+
+    block = lax.broadcasted_iota(jnp.int32, (16, 128), 1) // 32
+
+    def joined(parts):
+        result = parts[0]
+        for n in range(1, 4):
+            result = jnp.where(block == n, parts[n], result)
+        return result
+
+    def turn(value, shift):
+        return value if shift % 4 == 0 else pltpu.roll(value, 32 * (shift % 4), 1)
+
+    turned[...] = faces.T
+    for m in range(BLOCKS):
+        for parity in range(2):
+            t_faces[16 * m : 16 * m + 16, 128 * parity : 128 * parity + 128] = joined(
+                [
+                    turn(
+                        turned[
+                            32 * q + 16 * parity : 32 * q + 16 * parity + 16,
+                            128 * (m // 4) : 128 * (m // 4) + 128,
+                        ],
+                        q - m,
+                    )
+                    for q in range(4)
+                ]
+            )
+    modes = dot3((zbasis[0], zbasis[1]), halves(t_faces[...]))
     west_end = modes[:, :128] + modes[:, 128:]
     east_end = modes[:, :128] - modes[:, 128:]
 
-    meta_t = meta.T
-    facts = jnp.concatenate([meta_t[0:8]] * 4, axis=1)
-    stiff, allowed = facts[0:1], facts[1:2]
-    west_slot, east_slot = facts[2:3], facts[3:4]
-    lane = lax.broadcasted_iota(jnp.int32, (1, 128), 1)
-    column = (lane % 32).astype(F32)
-    offsets = [o for o in range(-REACH, REACH + 1) if o != 0]
-    west_hits = [
-        ((west_slot >= 0.0) & (column - west_slot == np.float32(o))).astype(F32) for o in offsets
-    ]
-    east_hits = [
-        ((east_slot >= 0.0) & (column - east_slot == np.float32(o))).astype(F32) for o in offsets
-    ]
-
-    def shifted(value, hits_by_offset):
-        parts = [
-            pltpu.roll(value, o % 128, 1) * hit for o, hit in zip(offsets, hits_by_offset)
-        ]
-        return ((parts[0] + parts[1]) + (parts[2] + parts[3])) + (parts[4] + parts[5])
-
-    def exchange(first, last):
-        return shifted(last, west_hits), shifted(first, east_hits)
-
-    face_near, face_far = end_responses(lam_z[...] + k_row / stiff, BX)
+    def by_lane(at):
+        values = [numbers[at + 128 * n : at + 128 * n + 128] for n in range(3)]
+        return jnp.where(stiff < 2.0, values[0], jnp.where(stiff < 8.0, values[1], values[2]))
+
+    face_near, face_far = by_lane(FACE_NEAR), by_lane(FACE_FAR)
     twice = (allowed > 1.0).astype(F32)
     west1, east1 = exchange(west_end, east_end)
     west1, east1 = west1 * twice, east1 * twice
@@ -414,18 +497,11 @@
     last = east_end + face_far * west1 + face_near * east1
     west2, east2 = exchange(first, last)
     moved = (west2 - west1) + (east2 - east1)
-    coarse = stiff * jnp.sum(moved * zsum[...], axis=0, keepdims=True)
-    diagonal = stiff * np.float32(2 * NZ + 2 * BX) + np.float32(BX * NZ) * k_row
-    target = jnp.broadcast_to(coarse / diagonal, (8, 128))
-    coupling = stiff * np.float32(NZ) / diagonal
-    both_hits = [coupling * (w + e) for w, e in zip(west_hits, east_hits)]
-    correction = DAMPING * target
-    for _ in range(CITERS - 1):
-        beside = shifted(correction, both_hits)
-        correction = correction + DAMPING * (target - correction + beside)
-    correction = correction[0:1]
-    west3 = west2 + zsum[...] * shifted(correction, west_hits)
-    east3 = east2 + zsum[...] * shifted(correction, east_hits)
+    coarse = stiff * jnp.sum(moved * zsum, axis=0, keepdims=True)
+    target = jnp.broadcast_to(DAMPING * coarse / diagonal, (16, 128))
+    corrections = dot3(halves(target), (passing[0], passing[1]))
+    west3 = west2 + zsum * corrections[0:1, :128]
+    east3 = east2 + zsum * corrections[0:1, 128:]
     first = west_end + face_near * west3 + face_far * east3
     last = east_end + face_far * west3 + face_near * east3
     west4, east4 = exchange(first, last)
@@ -433,28 +509,33 @@
     west = jnp.where(again, west4, west3)
     east = jnp.where(again, east4, east3)
     sums = jnp.concatenate((west + east, west - east), axis=1)
-    t_faces[...] = dot3(zbasis_t, halves(sums))
-
-    turned = jnp.concatenate(
-        [
-            jnp.concatenate(
-                [
-                    t_faces[16 * m : 16 * m + 16, 128 * parity + 32 * q : 128 * parity + 32 * q + 32]
-                    for q in range(4)
-                    for parity in range(2)
-                ],
-                axis=0,
-            )
-            for m in range(BLOCKS)
-        ],
-        axis=1,
-    )
-    faces = turned.T
+    t_faces[...] = dot3((zbasis[2], zbasis[3]), halves(sums))
+
+    for q in range(4):
+        for parity in range(2):
+            for h in range(2):
+                turned[
+                    32 * q + 16 * parity : 32 * q + 16 * parity + 16, 128 * h : 128 * h + 128
+                ] = joined(
+                    [
+                        turn(
+                            t_faces[
+                                64 * h + 16 * m : 64 * h + 16 * m + 16,
+                                128 * parity : 128 * parity + 128,
+                            ],
+                            m - q,
+                        )
+                        for m in range(4)
+                    ]
+                )
+    faces = turned[...].T
     for m in range(BLOCKS):
         out[pl.ds(96 * m + 2, 32, stride=3), :] = faces[32 * m : 32 * m + 32]
-    driven = jnp.zeros((256, 256), F32)
-    for level in range(3):
-        driven = driven + dot3(halves(jnp.where(hits[level], faces, 0.0)), links[level], NT)
+    levelled = [
+        jnp.concatenate([link[256 * n : 256 * n + 256, :] for n in range(3)], axis=1)
+        for link in links
+    ]
+    driven = dot3(spread(faces), levelled, NT)
     sides = interfaces(
         [even[m] + driven[32 * m : 32 * m + 32, 0:128] for m in range(BLOCKS)],
         [odd[m] + driven[32 * m : 32 * m + 32, 128:256] for m in range(BLOCKS)],
@@ -465,7 +546,7 @@
 
 
 def backward_kernel(
-    levels, inbox, w_in, back_h, back_l, th, tl, kq, out, features, sums, rows_out, sems,
+    levels, inbox, w_in, tables, kq, out, features, sums, rows_out, sems,
 ):
     easing = 1.0 / stiffness_scalar(levels[0])
     for kind in range(3):
@@ -489,7 +570,7 @@
                     pair.append(w + drive * inverted(base[half] + shift))
                 terms.append(halves(jnp.concatenate(pair, axis=0)))
             u = [jnp.concatenate([t[h] for t in terms], axis=0) for h in range(2)]
-            sums[q, 256 * parity : 256 * parity + 256, :] = dot3(u, (th[q], tl[q]), NT)
+            sums[q, 256 * parity : 256 * parity + 256, :] = dot3(u, (tables[q], tables[4 + q]), NT)
     copies = []
     for n in range(4):
         cut = slice(256 * n, 256 * n + 256)
@@ -506,7 +587,7 @@
                 f = jnp.concatenate((p1[:, half] + p5[:, half], mixed), axis=1)
                 terms.append(halves(e + f if n < 2 else e - f))
             v = [jnp.concatenate([t[h] for t in terms], axis=0) for h in range(2)]
-            sides.append(dot3((back_h[parity], back_l[parity]), v))
+            sides.append(dot3((tables[12 + parity], tables[14 + parity]), v))
         for k in range(16):
             rows = slice(16 * k, 16 * k + 16)
             rows_out[k, :, cut] = sides[0][rows] + sides[1][rows]
@@ -532,22 +613,22 @@
 GRANT = pltpu.CompilerParams(vmem_limit_bytes=20 * 2**20)
 
 
-def constants(back=False):
+def constants():
     tables = []
-    for table in (np.swapaxes(PLANE, 1, 2), T) if back else (PLANE, T):
-        tables.extend(jnp.asarray(t) for t in two_terms(table))
-    tables.append(jnp.asarray(KQ[None, :], F32))
-    return tables
+    for table in (T, PLANE, np.swapaxes(PLANE, 1, 2)):
+        tables.extend(two_terms(table))
+    return jnp.asarray(np.concatenate(tables)), jnp.asarray(KQ[None, :], F32)
 
 
 def run_forward(levels, neighbours, sweeps, mode, x, **kw):
     return pl.pallas_call(
         forward_kernel,
-        in_specs=[SMEM] * 4 + [HBM] * 5 + [VMEM],
-        out_specs=[VMEM, HBM],
+        in_specs=[SMEM] * 4 + [HBM] * 2 + [VMEM],
+        out_specs=[VMEM, HBM, VMEM],
         out_shape=[
             jax.ShapeDtypeStruct((768, 128), F32),
             jax.ShapeDtypeStruct((8, 256, 256), F32),
+            jax.ShapeDtypeStruct((8, 128), F32),
         ],
         scratch_shapes=[
             pltpu.VMEM((BX, ROWS, NY), F32),
@@ -570,38 +651,55 @@
     )(levels, neighbours, sweeps, mode, x, *constants())
 
 
-def run_columns(device, inbox, **kw):
-    lam_x = jnp.asarray(np.tile(LX[IX], 4)[None, :], F32)
-    lam_z = jnp.asarray(LZ[:, None], F32)
-    zbasis = [jnp.asarray(t) for table in (ZBASIS, ZBASIS.T) for t in two_terms(table)]
+def run_prepare(device, token, **kw):
+    zbasis = np.stack([t for table in (ZBASIS, ZBASIS.T) for t in two_terms(table)])
     tables = [
-        lam_x, lam_z, jnp.asarray(LINK_SCALE, F32), jnp.asarray(LINK_LAMBDA, F32), *zbasis,
+        jnp.asarray(np.tile(LX[IX], 4)[None, :], F32), jnp.asarray(LZ[:, None], F32),
+        jnp.asarray(LINK_SCALE, F32), jnp.asarray(LINK_LAMBDA, F32), jnp.asarray(zbasis),
         jnp.asarray(ZSUM, F32),
     ]
+    shapes = [((Z_SUM + 128, 128), F32), ((2048, 128), BF16)]
     return pl.pallas_call(
-        column_kernel,
+        prepare_kernel,
         grid_spec=pltpu.PrefetchScalarGridSpec(
             num_scalar_prefetch=1,
             grid=(1,),
             in_specs=[
-                whole((768, 128)),
+                whole((8, 128)),
                 pl.BlockSpec((1, 1, 128), lambda i, own: (own[0], 0, 0)),
             ]
             + [whole(t.shape) for t in tables],
-            out_specs=whole((768, 128)),
-            scratch_shapes=[pltpu.VMEM((256, 256), F32), pltpu.VMEM((128, 256), F32)],
+            out_specs=[VMEM] * len(shapes),
         ),
+        out_shape=[jax.ShapeDtypeStruct(*shape) for shape in shapes],
+        compiler_params=GRANT,
+        name="prepare",
+        **kw,
+    )(device, token, jnp.asarray(KQ_OWN, F32), *tables)
+
+
+def run_columns(inbox, prepared, **kw):
+    return pl.pallas_call(
+        column_kernel,
+        in_specs=[VMEM] * (1 + len(prepared)),
+        out_specs=VMEM,
+        scratch_shapes=[
+            pltpu.VMEM((256, 256), F32),
+            pltpu.VMEM((128, 256), F32),
+            pltpu.VMEM((128, 256), F32),
+            pltpu.VMEM((2, 128, 256), BF16),
+        ],
         out_shape=jax.ShapeDtypeStruct((768, 128), F32),
+        compiler_params=GRANT,
         name="columns",
         **kw,
-    )(device, inbox, jnp.asarray(KQ_OWN, F32), *tables)
+    )(inbox, *prepared)
 
 
 def run_backward(levels, inbox, w, **kw):
-    tables = constants(True)
     return pl.pallas_call(
         backward_kernel,
-        in_specs=[SMEM] + [VMEM] * (2 + len(tables)),
+        in_specs=[SMEM] + [VMEM] * 4,
         out_specs=HBM,
         out_shape=jax.ShapeDtypeStruct((BX, ROWS, NY), F32),
         scratch_shapes=[
@@ -613,7 +711,7 @@
         compiler_params=GRANT,
         name="backward",
         **kw,
-    )(levels, inbox, w, *tables)
+    )(levels, inbox, w, *constants())
 
 
 def traded(outbox):
@@ -625,8 +723,8 @@
 def body(divergence, neighbours, levels, sweeps):
     mode = lax.axis_index("mode").astype(jnp.int32)
     device = mode * 32 + lax.axis_index("blk").astype(jnp.int32)
-    outbox, w = run_forward(levels, neighbours, sweeps, mode[None], divergence[0])
-    outbox = run_columns(device[None], traded(outbox))
+    outbox, w, token = run_forward(levels, neighbours, sweeps, mode[None], divergence[0])
+    outbox = run_columns(traded(outbox), run_prepare(device[None], token))
     return run_backward(levels, traded(outbox), w)[None]
 
 

time: 74.8 us -> 72.6 us (0.971)
  local copies, waits for them, and re-layouts: 0.98 us -> 8.22 us
  waiting for transfers between devices: 16.7 us -> 10.2 us
  Pallas kernels: 15.6 us -> 13.6 us
  starting transfers between devices: 16.5 us -> 15.7 us
    unnamed x12 -> x22, local copies, waits for them, and re-layouts: 0.98 us -> 8.22 us
    all_to_all x1, waiting for transfers between devices: 16.7 us -> 10.2 us  [traded(): lax.all_to_all(pieces, ('mode', 'blk'), split_axis=0, concat_axis=0, tile...]
    pallas_call x3 -> x4, Pallas kernels: 15.6 us -> 13.6 us  [the longest x1 6.79 us: run_forward(): pl.pallas_call(forward_kernel, in_specs=[SMEM] * 4 + [HBM] * 2 + [VMEM],...]
    all_to_all x1, starting transfers between devices: 16.5 us -> 15.7 us  [traded(): lax.all_to_all(pieces, ('mode', 'blk'), split_axis=0, concat_axis=0, tile...]
where the time goes in v2:
time: 72.6 us; the launch traced here: 72.1 us
  blocking collectives  23.8 us (33%)
  starting transfers between devices  15.7 us (22%)
  Pallas kernels  13.6 us (19%)
  waiting for transfers between devices  10.2 us (14%)
  local copies, waits for them, and re-layouts  8.22 us (11%)
  between operations  0.73 us (1%)
    all_to_all x1, blocking collectives, traded(): lax.all_to_all(pieces, ('mode', 'blk'), split_axis=0, concat_axis=0, tile...  23.8 us
    all_to_all x1, starting transfers between devices, traded(): lax.all_to_all(pieces, ('mode', 'blk'), split_axis=0, concat_axis=0, tile...  15.7 us
    all_to_all x1, waiting for transfers between devices, traded(): lax.all_to_all(pieces, ('mode', 'blk'), split_axis=0, concat_axis=0, tile...  10.2 us
    unnamed x22, local copies, waits for them, and re-layouts  8.22 us
    pallas_call x1, Pallas kernels, run_forward(): pl.pallas_call(forward_kernel, in_specs=[SMEM] * 4 + [HBM] * 2 + [VMEM],...  6.79 us
    pallas_call x1, Pallas kernels, run_backward(): pl.pallas_call(backward_kernel, in_specs=[SMEM] + [VMEM] * 4, out_specs=H...  3.42 us
    pallas_call x1, Pallas kernels, run_columns(): pl.pallas_call(column_kernel, in_specs=[VMEM] * (1 + len(prepared)), out_...  3.02 us
  transfers between devices with their start and end apart: 1, of which 1 were waited for; matrix products, arithmetic and copies ran while one was open for 0% of the time, Pallas kernels for 0%

profile of v2, /device:TPU:1, one launch (start us, length us, event | category | flops | bytes accessed | tf_op | source)
XLA Modules:
  0.0 72.1 jit_solution(5879236433252490326)
XLA Ops:
  0.7 0.0 copy-start.8
  0.7 6.8 %forward.1 = (f32[768,128]{1,0:T(8,128)}, f32[8,256,256]{2,1,0:T(8,128)}, f32[8,128]{1,0:T(8,128)}) custom-call(s32[1]{0:T(128)S(6)} %copy.18.levels, s32[1,2]{1,0:T(1,128)} %neighbours.1, s32[3]{0:T(128)} %sweeps.1, s32[1]{0:T(128)} %bitcast.mode, f32[32,16,1024]{2,1,0:T(8,128)} %bitcast.11, bf16[16,256,256]{2,1,0:T(8,128)(2,1)} %constant.29.clone.tables_in.tables, ...), custom_call_target="tpu_custom_call" | custom-call | tf_op jit(solution)/shard_map/forward/pallas_call | solution.py:624
  7.5 0.0 copy-start
  7.5 15.7 %all-to-all-start = ((f32[256,1,384]{2,1,0:T(1,128)}), f32[256,1,384]{2,1,0:T(1,128)S(1)}, u32[]{:S(2)}, u32[]{:S(2)}) async-start(f32[256,1,384]{2,1,0:T(1,128)} %bitcast.12), calls=%async_computation | async-start | bytes 786432 | tf_op jit(solution)/shard_map/all_to_all | solution.py:719
  23.1 0.0 copy-start.2
  23.2 0.9 %copy-done.2 = f32[256,1,128]{2,1,0:T(1,128)S(1)} copy-done((f32[256,1,128]{2,1,0:T(1,128)S(1)}, f32[256,1,128]{2,1,0:T(1,128)}, u32[]{:S(2)}) %copy-start.2) | copy-done | bytes 131096
  24.1 0.0 copy-start.3
  24.1 0.9 %copy-done.3 = bf16[4,128,128]{2,1,0:T(8,128)(2,1)S(1)} copy-done((bf16[4,128,128]{2,1,0:T(8,128)(2,1)S(1)}, bf16[4,128,128]{2,1,0:T(8,128)(2,1)}, u32[]{:S(2)}) %copy-start.3) | copy-done | bytes 131096
  25.0 0.0 copy-start.4
  25.0 0.9 %copy-done.4 = f32[256,128]{1,0:T(8,128)S(1)} copy-done((f32[256,128]{1,0:T(8,128)S(1)}, f32[256,128]{1,0:T(8,128)}, u32[]{:S(2)}) %copy-start.4) | copy-done | bytes 131096
  25.9 0.0 copy-start.5
  25.9 0.9 %copy-done.5 = f32[256,128]{1,0:T(8,128)S(1)} copy-done((f32[256,128]{1,0:T(8,128)S(1)}, f32[256,128]{1,0:T(8,128)}, u32[]{:S(2)}) %copy-start.5) | copy-done | bytes 131096
  26.8 0.0 copy-start.6
  26.8 0.8 %copy-done.6 = f32[128,1]{1,0:T(8,128)S(1)} copy-done((f32[128,1]{1,0:T(8,128)S(1)}, f32[128,1]{1,0:T(8,128)}, u32[]{:S(2)}) %copy-start.6) | copy-done | bytes 536
  27.6 0.0 copy-start.7
  27.6 0.8 %copy-done.7 = f32[128,1]{1,0:T(8,128)S(1)} copy-done((f32[128,1]{1,0:T(8,128)S(1)}, f32[128,1]{1,0:T(8,128)}, u32[]{:S(2)}) %copy-start.7) | copy-done | bytes 536
  28.4 0.0 copy-start.9
  28.5 0.7 copy-done.9
  29.1 0.0 copy-start.10
  29.1 0.7 copy-done.10
  29.8 0.3 prepare.1
  30.1 10.2 %all-to-all-done = f32[256,1,384]{2,1,0:T(1,128)S(1)} async-done(((f32[256,1,384]{2,1,0:T(1,128)}), f32[256,1,384]{2,1,0:T(1,128)S(1)}, u32[]{:S(2)}, u32[]{:S(2)}) %all-to-all-start) | async-done | bytes 393248 | tf_op jit(solution)/shard_map/all_to_all | solution.py:719
  40.3 3.0 %columns.1 = f32[768,128]{1,0:T(8,128)S(1)} custom-call(f32[768,128]{1,0:T(8,128)S(1)} %bitcast.8, f32[1048,128]{1,0:T(8,128)S(1)} %get-tuple-element.12.numbers, bf16[2048,128]{1,0:T(8,128)(2,1)S(1)} %get-tuple-element.13.terms_in), custom_call_target="tpu_custom_call" | custom-call | tf_op jit(solution)/shard_map/columns/pallas_call | solution.py:682
  43.4 23.8 %all_to_all.10 = f32[256,1,384]{2,1,0:T(1,128)S(1)} all-to-all(f32[256,1,384]{2,1,0:T(1,128)S(1)} %bitcast.10), channel_id=1, replica_groups=mesh['mode'=8,'blk'=32] {'mode','blk'}, dimensions={0} | all-to-all | bytes 786432 | tf_op jit(solution)/shard_map/all_to_all | solution.py:719
  67.1 0.0 copy-done.8
  67.1 0.0 copy-done
  67.1 0.0 copy-start.1
  67.1 1.6 %copy-done.1 = f32[8,256,256]{2,1,0:T(8,128)S(1)} copy-done((f32[8,256,256]{2,1,0:T(8,128)S(1)}, f32[8,256,256]{2,1,0:T(8,128)}, u32[]{:S(2)}) %copy-start.1) | copy-done | bytes 2097176
  68.7 3.4 %backward.1 = f32[32,16,1024]{2,1,0:T(8,128)} custom-call(s32[1]{0:T(128)S(6)} %copy.18.levels, f32[768,128]{1,0:T(8,128)S(1)} %bitcast.9, f32[8,256,256]{2,1,0:T(8,128)S(1)} %copy-done.1, bf16[16,256,256]{2,1,0:T(8,128)(2,1)S(1)} %copy-done, f32[1,1024]{1,0:T(1,128)S(1)} %copy-done.8), custom_call_target="tpu_custom_call" | custom-call | tf_op jit(solution)/shard_map/backward/pallas_call | solution.py:700
Async XLA Ops:
  0.7 66.5 %copy-start.8 = (f32[1,1024]{1,0:T(1,128)S(1)}, f32[1,1024]{1,0:T(1,128)}, u32[]{:S(2)}) copy-start(f32[1,1024]{1,0:T(1,128)} %constant.30.clone.kq) | copy-start | bytes 12292
  7.5 59.7 %copy-start = (bf16[16,256,256]{2,1,0:T(8,128)(2,1)S(1)}, bf16[16,256,256]{2,1,0:T(8,128)(2,1)}, u32[]{:S(2)}) copy-start(bf16[16,256,256]{2,1,0:T(8,128)(2,1)} %constant.29.clone.tables_in.tables) | copy-start | bytes 6291460
  7.5 32.9 %all-to-all-start = ((f32[256,1,384]{2,1,0:T(1,128)}), f32[256,1,384]{2,1,0:T(1,128)S(1)}, u32[]{:S(2)}, u32[]{:S(2)}) async-start(f32[256,1,384]{2,1,0:T(1,128)} %bitcast.12), calls=%async_computation | async-start | bytes 786432 | tf_op jit(solution)/shard_map/all_to_all | solution.py:719
  23.1 0.9 %copy-start.2 = (f32[256,1,128]{2,1,0:T(1,128)S(1)}, f32[256,1,128]{2,1,0:T(1,128)}, u32[]{:S(2)}) copy-start(f32[256,1,128]{2,1,0:T(1,128)} %constant.37.clone.k_own) | copy-start | bytes 393220
  24.1 0.9 %copy-start.3 = (bf16[4,128,128]{2,1,0:T(8,128)(2,1)S(1)}, bf16[4,128,128]{2,1,0:T(8,128)(2,1)}, u32[]{:S(2)}) copy-start(bf16[4,128,128]{2,1,0:T(8,128)(2,1)} %constant.35.clone.zbasis) | copy-start | bytes 393220
  25.0 0.9 %copy-start.4 = (f32[256,128]{1,0:T(8,128)S(1)}, f32[256,128]{1,0:T(8,128)}, u32[]{:S(2)}) copy-start(f32[256,128]{1,0:T(8,128)} %constant.34.clone.link_lambda) | copy-start | bytes 393220
  25.9 0.9 %copy-start.5 = (f32[256,128]{1,0:T(8,128)S(1)}, f32[256,128]{1,0:T(8,128)}, u32[]{:S(2)}) copy-start(f32[256,128]{1,0:T(8,128)} %constant.33.clone.link_scale) | copy-start | bytes 393220
  26.8 0.8 %copy-start.6 = (f32[128,1]{1,0:T(8,128)S(1)}, f32[128,1]{1,0:T(8,128)}, u32[]{:S(2)}) copy-start(f32[128,1]{1,0:T(8,128)} %constant.36.clone.zsum) | copy-start | bytes 1540
  27.6 0.8 %copy-start.7 = (f32[128,1]{1,0:T(8,128)S(1)}, f32[128,1]{1,0:T(8,128)}, u32[]{:S(2)}) copy-start(f32[128,1]{1,0:T(8,128)} %constant.32.clone.lam_z) | copy-start | bytes 1540
  28.4 0.7 copy-start.9
  29.1 0.7 copy-start.10
  67.1 1.6 %copy-start.1 = (f32[8,256,256]{2,1,0:T(8,128)S(1)}, f32[8,256,256]{2,1,0:T(8,128)}, u32[]{:S(2)}) copy-start(f32[8,256,256]{2,1,0:T(8,128)} %get-tuple-element.14.w_in) | copy-start | bytes 6291460

commit v3 on v2

--- a/solution.py
+++ b/solution.py
@@ -153,7 +153,7 @@
 
 def forward_kernel(
     levels, neighbours, sweeps, mode, x, tables_in, kq,
-    out, w_out, token, x_buffer, p_h, p_l, t_h, t_l, yh, yl, fh, fl, w_buffer, features,
+    out, w_out, x_buffer, p_h, p_l, t_h, t_l, yh, yl, fh, fl, w_buffer, features,
     x_sems, t_sems, w_sems,
 ):
     tables = [
@@ -165,13 +165,10 @@
             )
         )
     ]
-    token[...] = jnp.zeros((8, 128), F32)
-    for copy in pieces_of(x, x_buffer, x_sems, 0) + tables[:2]:
-        copy.start()
-    for step in range(1, 4):
+    for step in range(4):
         for copy in pieces_of(x, x_buffer, x_sems, step):
             copy.start()
-    for copy in tables[2:]:
+    for copy in tables:
         copy.start()
 
     def fold(step, k):
@@ -191,37 +188,29 @@
                     jnp.concatenate((f0 + turn0, g0 + turn1), axis=1),
                     jnp.concatenate((f0 - turn0, g0 - turn1), axis=1),
                 )
-                rows = slice(128 * step + 64 * parity + 16 * k, 128 * step + 64 * parity + 16 * k + 16)
+                at = 256 * parity + 16 * (4 * step + k)
+                rows = slice(at, at + 16)
                 for q in range(4):
                     high, low = halves(parts[q])
                     yh[q, rows, :] = high
                     yl[q, rows, :] = low
 
-    def transform(step, q):
-        rows = slice(128 * step, 128 * step + 128)
-        for q in (q,):
+    def transform(q):
+        for parity in range(2):
+            rows = slice(256 * parity, 256 * parity + 256)
             f = dot3((yh[q, rows, :], yl[q, rows, :]), (t_h[q], t_l[q]))
-            for parity in range(2):
-                place = slice(256 * parity + 64 * step, 256 * parity + 64 * step + 64)
-                high, low = halves(f[64 * parity : 64 * parity + 64])
-                fh[q, place, :] = high
-                fl[q, place, :] = low
+            high, low = halves(f)
+            fh[q, rows, :] = high
+            fl[q, rows, :] = low
 
     for step in range(4):
         for copy in pieces_of(x, x_buffer, x_sems, step):
             copy.wait()
-        if step == 1:
-            for copy in tables[:2]:
-                copy.wait()
         if step == 3:
-            for copy in tables[2:]:
+            for copy in tables:
                 copy.wait()
         for k in range(4):
             fold(step, k)
-            if step > 0:
-                transform(step - 1, k)
-    for q in range(4):
-        transform(3, q)
     level = levels[0]
     stiffness = stiffness_scalar(level)
     lambdas = [stiffness * column for column in per_mode(LB)]
@@ -249,7 +238,10 @@
         return values[0]
 
     copies = []
+    transform(0)
     for q in range(4):
+        if q < 3:
+            transform(q + 1)
         base = [column + kq[:, 256 * q : 256 * q + 256] for column in lambdas]
         for parity in range(2):
             rows = slice(256 * parity, 256 * parity + 256)
@@ -315,16 +307,17 @@
 RATIOS, SCALES, NEAR_FAR, FACE_NEAR, FACE_FAR, Z_SUM = 8, 72, 136, 152, 536, 920
 
 
-def prepare_kernel(
-    own, token, k_own, lam_x, lam_z, link_scale, link_lambda, zbasis, zsum,
-    numbers, terms,
-):
-    del own, token
+def prepare_kernel(own, w_in, k_own, constants_in, zbasis, numbers, terms, w_out, sem):
+    del own
+    copy = pltpu.make_async_copy(w_in, w_out, sem)
+    copy.start()
+    link_scale, link_lambda = constants_in[0:256], constants_in[256:512]
+    zsum, lam_z, lam_x = constants_in[512:640], constants_in[640:768], constants_in[768:776]
     k_row = k_own[0]
     numbers[0:8] = jnp.broadcast_to(k_row, (8, 128))
     level = lax.broadcasted_iota(jnp.int32, (8, 128), 0)
     easing = jnp.where(level == 0, 1.0, jnp.where(level == 1, 0.25, 0.0625))
-    near, far = end_responses(lam_x[...] + k_row * easing, ROWS)
+    near, far = end_responses(lam_x + k_row * easing, ROWS)
     numbers[NEAR_FAR : NEAR_FAR + 8] = near
     numbers[NEAR_FAR + 8 : NEAR_FAR + 16] = far
     carry = jnp.zeros((8, 128), F32)
@@ -335,15 +328,16 @@
         carry = near + far * far * carry * scale
     for level in range(3):
         shift = k_row * np.float32(0.25**level)
-        face_near, face_far = end_responses(lam_z[...] + shift, BX)
+        face_near, face_far = end_responses(lam_z + shift, BX)
         numbers[FACE_NEAR + 128 * level : FACE_NEAR + 128 * level + 128] = face_near
         numbers[FACE_FAR + 128 * level : FACE_FAR + 128 * level + 128] = face_far
-        high, low = halves(link_scale[...] / (link_lambda[...] + shift))
+        high, low = halves(link_scale / (link_lambda + shift))
         terms[256 * level : 256 * level + 256] = high
         terms[768 + 256 * level : 768 + 256 * level + 256] = low
     for n in range(4):
         terms[1536 + 128 * n : 1536 + 128 * n + 128] = zbasis[n]
-    numbers[Z_SUM : Z_SUM + 128] = jnp.broadcast_to(zsum[...], (128, 128))
+    numbers[Z_SUM : Z_SUM + 128] = zsum
+    copy.wait()
 
 
 def column_kernel(
@@ -624,11 +618,10 @@
     return pl.pallas_call(
         forward_kernel,
         in_specs=[SMEM] * 4 + [HBM] * 2 + [VMEM],
-        out_specs=[VMEM, HBM, VMEM],
+        out_specs=[VMEM, HBM],
         out_shape=[
             jax.ShapeDtypeStruct((768, 128), F32),
             jax.ShapeDtypeStruct((8, 256, 256), F32),
-            jax.ShapeDtypeStruct((8, 128), F32),
         ],
         scratch_shapes=[
             pltpu.VMEM((BX, ROWS, NY), F32),
@@ -651,37 +644,41 @@
     )(levels, neighbours, sweeps, mode, x, *constants())
 
 
-def run_prepare(device, token, **kw):
+def run_prepare(device, w, **kw):
     zbasis = np.stack([t for table in (ZBASIS, ZBASIS.T) for t in two_terms(table)])
-    tables = [
-        jnp.asarray(np.tile(LX[IX], 4)[None, :], F32), jnp.asarray(LZ[:, None], F32),
-        jnp.asarray(LINK_SCALE, F32), jnp.asarray(LINK_LAMBDA, F32), jnp.asarray(zbasis),
-        jnp.asarray(ZSUM, F32),
-    ]
-    shapes = [((Z_SUM + 128, 128), F32), ((2048, 128), BF16)]
+    wide = np.ones((1, 128))
+    numbers = np.concatenate(
+        (
+            LINK_SCALE, LINK_LAMBDA, ZSUM * wide, LZ[:, None] * wide,
+            np.tile(LX[IX], 4)[None, :] * np.ones((8, 1)),
+        )
+    )
+    shapes = [((Z_SUM + 128, 128), F32), ((2048, 128), BF16), (w.shape, F32)]
     return pl.pallas_call(
         prepare_kernel,
         grid_spec=pltpu.PrefetchScalarGridSpec(
             num_scalar_prefetch=1,
             grid=(1,),
             in_specs=[
-                whole((8, 128)),
+                HBM,
                 pl.BlockSpec((1, 1, 128), lambda i, own: (own[0], 0, 0)),
-            ]
-            + [whole(t.shape) for t in tables],
+                whole(numbers.shape),
+                whole(zbasis.shape),
+            ],
             out_specs=[VMEM] * len(shapes),
+            scratch_shapes=[pltpu.SemaphoreType.DMA],
         ),
         out_shape=[jax.ShapeDtypeStruct(*shape) for shape in shapes],
         compiler_params=GRANT,
         name="prepare",
         **kw,
-    )(device, token, jnp.asarray(KQ_OWN, F32), *tables)
-
-
-def run_columns(inbox, prepared, **kw):
+    )(device, w, jnp.asarray(KQ_OWN, F32), jnp.asarray(numbers, F32), jnp.asarray(zbasis))
+
+
+def run_columns(inbox, numbers, terms, **kw):
     return pl.pallas_call(
         column_kernel,
-        in_specs=[VMEM] * (1 + len(prepared)),
+        in_specs=[VMEM] * 3,
         out_specs=VMEM,
         scratch_shapes=[
             pltpu.VMEM((256, 256), F32),
@@ -693,7 +690,7 @@
         compiler_params=GRANT,
         name="columns",
         **kw,
-    )(inbox, *prepared)
+    )(inbox, numbers, terms)
 
 
 def run_backward(levels, inbox, w, **kw):
@@ -723,8 +720,9 @@
 def body(divergence, neighbours, levels, sweeps):
     mode = lax.axis_index("mode").astype(jnp.int32)
     device = mode * 32 + lax.axis_index("blk").astype(jnp.int32)
-    outbox, w, token = run_forward(levels, neighbours, sweeps, mode[None], divergence[0])
-    outbox = run_columns(traded(outbox), run_prepare(device[None], token))
+    outbox, w = run_forward(levels, neighbours, sweeps, mode[None], divergence[0])
+    numbers, terms, w = run_prepare(device[None], w)
+    outbox = run_columns(traded(outbox), numbers, terms)
     return run_backward(levels, traded(outbox), w)[None]
 
 

time: 72.6 us -> 70.7 us (0.974)
  local copies, waits for them, and re-layouts: 8.22 us -> 5.72 us
  waiting for transfers between devices: 10.2 us -> 11 us
    unnamed x22 -> x16, local copies, waits for them, and re-layouts: 8.22 us -> 5.72 us
    all_to_all x1, waiting for transfers between devices: 10.2 us -> 11 us  [traded(): lax.all_to_all(pieces, ('mode', 'blk'), split_axis=0, concat_axis=0, tile...]
  transfers between devices with their start and end apart: 1 -> 1, of which waited for: 1 -> 1; matrix products, arithmetic and copies ran while one was open for 0% -> 0% of each run, Pallas kernels for 0% -> 1%
where the time goes in v3:
time: 70.7 us; the launch traced here: 70.4 us
  blocking collectives  23.8 us (34%)
  starting transfers between devices  15.7 us (22%)
  Pallas kernels  13.5 us (19%)
  waiting for transfers between devices  11 us (16%)
  local copies, waits for them, and re-layouts  5.72 us (8%)
  between operations  0.72 us (1%)
    all_to_all x1, blocking collectives, traded(): lax.all_to_all(pieces, ('mode', 'blk'), split_axis=0, concat_axis=0, tile...  23.8 us
    all_to_all x1, starting transfers between devices, traded(): lax.all_to_all(pieces, ('mode', 'blk'), split_axis=0, concat_axis=0, tile...  15.7 us
    all_to_all x1, waiting for transfers between devices, traded(): lax.all_to_all(pieces, ('mode', 'blk'), split_axis=0, concat_axis=0, tile...  11 us
    pallas_call x1, Pallas kernels, run_forward(): pl.pallas_call(forward_kernel, in_specs=[SMEM] * 4 + [HBM] * 2 + [VMEM],...  6.7 us
    unnamed x16, local copies, waits for them, and re-layouts  5.72 us
    pallas_call x1, Pallas kernels, run_backward(): pl.pallas_call(backward_kernel, in_specs=[SMEM] + [VMEM] * 4, out_specs=H...  3.38 us
    pallas_call x1, Pallas kernels, run_columns(): pl.pallas_call(column_kernel, in_specs=[VMEM] * 3, out_specs=VMEM, scratc...  3.02 us
  transfers between devices with their start and end apart: 1, of which 1 were waited for; matrix products, arithmetic and copies ran while one was open for 0% of the time, Pallas kernels for 1%

profile of v3, /device:TPU:1, one launch (start us, length us, event | category | flops | bytes accessed | tf_op | source)
XLA Modules:
  0.0 70.4 jit_solution(13862093777026523753)
XLA Ops:
  0.7 6.7 %forward.1 = (f32[768,128]{1,0:T(8,128)}, f32[8,256,256]{2,1,0:T(8,128)}) custom-call(s32[1]{0:T(128)S(6)} %copy.14.levels, s32[1,2]{1,0:T(1,128)} %neighbours.1, s32[3]{0:T(128)} %sweeps.1, s32[1]{0:T(128)} %bitcast.mode, f32[32,16,1024]{2,1,0:T(8,128)} %bitcast.11, bf16[16,256,256]{2,1,0:T(8,128)(2,1)} %constant.21.clone.tables_in.tables, ...), custom_call_target="tpu_custom_call" | custom-call | tf_op jit(solution)/shard_map/forward/pallas_call | solution.py:618
  7.4 15.7 %all-to-all-start = ((f32[256,1,384]{2,1,0:T(1,128)}), f32[256,1,384]{2,1,0:T(1,128)S(1)}, u32[]{:S(2)}, u32[]{:S(2)}) async-start(f32[256,1,384]{2,1,0:T(1,128)} %bitcast.12), calls=%async_computation | async-start | bytes 786432 | tf_op jit(solution)/shard_map/all_to_all | solution.py:716
  23.0 0.0 copy-start.3
  23.0 1.6 %copy-done.3 = f32[8,256,256]{2,1,0:T(8,128)S(1)} copy-done((f32[8,256,256]{2,1,0:T(8,128)S(1)}, f32[8,256,256]{2,1,0:T(8,128)}, u32[]{:S(2)}) %copy-start.3) | copy-done | bytes 2097176
  24.6 0.0 copy-start.4
  24.6 1.0 %copy-done.4 = f32[776,128]{1,0:T(8,128)S(1)} copy-done((f32[776,128]{1,0:T(8,128)S(1)}, f32[776,128]{1,0:T(8,128)}, u32[]{:S(2)}) %copy-start.4) | copy-done | bytes 397336
  25.6 0.0 copy-start.5
  25.6 0.9 %copy-done.5 = bf16[4,128,128]{2,1,0:T(8,128)(2,1)S(1)} copy-done((bf16[4,128,128]{2,1,0:T(8,128)(2,1)S(1)}, bf16[4,128,128]{2,1,0:T(8,128)(2,1)}, u32[]{:S(2)}) %copy-start.5) | copy-done | bytes 131096
  26.5 0.0 copy-start.6
  26.5 0.9 %copy-done.6 = f32[256,1,128]{2,1,0:T(1,128)S(1)} copy-done((f32[256,1,128]{2,1,0:T(1,128)S(1)}, f32[256,1,128]{2,1,0:T(1,128)}, u32[]{:S(2)}) %copy-start.6) | copy-done | bytes 131096
  27.4 0.0 copy-start
  27.4 0.0 copy-start.7
  27.4 0.4 prepare.1
  27.9 0.0 copy-start.1
  27.9 1.3 %copy-done.1 = f32[8,256,256]{2,1,0:T(8,128)} copy-done((f32[8,256,256]{2,1,0:T(8,128)}, f32[8,256,256]{2,1,0:T(8,128)S(1)}, u32[]{:S(2)}) %copy-start.1) | copy-done | bytes 2097176
  29.2 11.0 %all-to-all-done = f32[256,1,384]{2,1,0:T(1,128)S(1)} async-done(((f32[256,1,384]{2,1,0:T(1,128)}), f32[256,1,384]{2,1,0:T(1,128)S(1)}, u32[]{:S(2)}, u32[]{:S(2)}) %all-to-all-start) | async-done | bytes 393248 | tf_op jit(solution)/shard_map/all_to_all | solution.py:716
  40.2 0.0 copy-start.2
  40.2 3.0 %columns.1 = f32[768,128]{1,0:T(8,128)S(1)} custom-call(f32[768,128]{1,0:T(8,128)S(1)} %bitcast.8, f32[1048,128]{1,0:T(8,128)S(1)} %get-tuple-element.12.numbers, bf16[2048,128]{1,0:T(8,128)(2,1)S(1)} %get-tuple-element.13.terms_in), custom_call_target="tpu_custom_call" | custom-call | tf_op jit(solution)/shard_map/columns/pallas_call | solution.py:679
  43.2 23.8 %all_to_all.10 = f32[256,1,384]{2,1,0:T(1,128)S(1)} all-to-all(f32[256,1,384]{2,1,0:T(1,128)S(1)} %bitcast.10), channel_id=1, replica_groups=mesh['mode'=8,'blk'=32] {'mode','blk'}, dimensions={0} | all-to-all | bytes 786432 | tf_op jit(solution)/shard_map/all_to_all | solution.py:716
  67.0 0.0 copy-done
  67.0 0.0 copy-done.7
  67.0 0.0 copy-done.2
  67.0 3.4 %backward.1 = f32[32,16,1024]{2,1,0:T(8,128)} custom-call(s32[1]{0:T(128)S(6)} %copy.14.levels, f32[768,128]{1,0:T(8,128)S(1)} %bitcast.9, f32[8,256,256]{2,1,0:T(8,128)S(1)} %copy-done.2, bf16[16,256,256]{2,1,0:T(8,128)(2,1)S(1)} %copy-done, f32[1,1024]{1,0:T(1,128)S(1)} %copy-done.7), custom_call_target="tpu_custom_call" | custom-call | tf_op jit(solution)/shard_map/backward/pallas_call | solution.py:697
Async XLA Ops:
  7.4 32.9 %all-to-all-start = ((f32[256,1,384]{2,1,0:T(1,128)}), f32[256,1,384]{2,1,0:T(1,128)S(1)}, u32[]{:S(2)}, u32[]{:S(2)}) async-start(f32[256,1,384]{2,1,0:T(1,128)} %bitcast.12), calls=%async_computation | async-start | bytes 786432 | tf_op jit(solution)/shard_map/all_to_all | solution.py:716
  23.0 1.6 %copy-start.3 = (f32[8,256,256]{2,1,0:T(8,128)S(1)}, f32[8,256,256]{2,1,0:T(8,128)}, u32[]{:S(2)}) copy-start(f32[8,256,256]{2,1,0:T(8,128)} %get-tuple-element.11.w_in) | copy-start | bytes 6291460
  24.6 1.0 %copy-start.4 = (f32[776,128]{1,0:T(8,128)S(1)}, f32[776,128]{1,0:T(8,128)}, u32[]{:S(2)}) copy-start(f32[776,128]{1,0:T(8,128)} %constant.24.clone.constants_in) | copy-start | bytes 1191940
  25.6 0.9 %copy-start.5 = (bf16[4,128,128]{2,1,0:T(8,128)(2,1)S(1)}, bf16[4,128,128]{2,1,0:T(8,128)(2,1)}, u32[]{:S(2)}) copy-start(bf16[4,128,128]{2,1,0:T(8,128)(2,1)} %constant.25.clone.zbasis) | copy-start | bytes 393220
  26.5 0.9 %copy-start.6 = (f32[256,1,128]{2,1,0:T(1,128)S(1)}, f32[256,1,128]{2,1,0:T(1,128)}, u32[]{:S(2)}) copy-start(f32[256,1,128]{2,1,0:T(1,128)} %constant.23.clone.k_own) | copy-start | bytes 393220
  27.4 39.6 %copy-start = (bf16[16,256,256]{2,1,0:T(8,128)(2,1)S(1)}, bf16[16,256,256]{2,1,0:T(8,128)(2,1)}, u32[]{:S(2)}) copy-start(bf16[16,256,256]{2,1,0:T(8,128)(2,1)} %constant.21.clone.tables_in.tables) | copy-start | bytes 6291460
  27.4 39.6 %copy-start.7 = (f32[1,1024]{1,0:T(1,128)S(1)}, f32[1,1024]{1,0:T(1,128)}, u32[]{:S(2)}) copy-start(f32[1,1024]{1,0:T(1,128)} %constant.22.clone.kq) | copy-start | bytes 12292
  27.9 1.3 %copy-start.1 = (f32[8,256,256]{2,1,0:T(8,128)}, f32[8,256,256]{2,1,0:T(8,128)S(1)}, u32[]{:S(2)}) copy-start(f32[8,256,256]{2,1,0:T(8,128)S(1)} %get-tuple-element.14.w_in) | copy-start | bytes 6291460
  40.2 26.8 %copy-start.2 = (f32[8,256,256]{2,1,0:T(8,128)S(1)}, f32[8,256,256]{2,1,0:T(8,128)}, u32[]{:S(2)}) copy-start(f32[8,256,256]{2,1,0:T(8,128)} %copy-done.1) | copy-start | bytes 6291460

commit v4 on v3

--- a/solution.py
+++ b/solution.py
@@ -153,7 +153,7 @@
 
 def forward_kernel(
     levels, neighbours, sweeps, mode, x, tables_in, kq,
-    out, w_out, x_buffer, p_h, p_l, t_h, t_l, yh, yl, fh, fl, w_buffer, features,
+    out_hbm, w_out, out, x_buffer, p_h, p_l, t_h, t_l, yh, yl, fh, fl, w_buffer, features,
     x_sems, t_sems, w_sems,
 ):
     tables = [
@@ -207,7 +207,7 @@
         for copy in pieces_of(x, x_buffer, x_sems, step):
             copy.wait()
         if step == 3:
-            for copy in tables:
+            for copy in tables[:2]:
                 copy.wait()
         for k in range(4):
             fold(step, k)
@@ -239,6 +239,8 @@
 
     copies = []
     transform(0)
+    for copy in tables[2:]:
+        copy.wait()
     for q in range(4):
         if q < 3:
             transform(q + 1)
@@ -265,11 +267,9 @@
                     features[half, at : at + 8, :] = summed(ends[half])
             for half in range(2):
                 features[2, place + 8 * half : place + 8 * half + 8, :] = totals[half]
-        if q % 2 == 1:
-            copy = pltpu.make_async_copy(
-                w_buffer.at[pl.ds(4 * (q // 2), 4)], w_out.at[pl.ds(4 * (q // 2), 4)],
-                w_sems.at[q // 2],
-            )
+        if q >= 2:
+            span = pl.ds(0, 6) if q == 2 else pl.ds(6, 2)
+            copy = pltpu.make_async_copy(w_buffer.at[span], w_out.at[span], w_sems.at[q - 2])
             copy.start()
             copies.append(copy)
     last = mode[0] == BLOCKS - 1
@@ -288,6 +288,9 @@
     out[pl.ds(0, DEVICES, stride=3), :] = jnp.where(last, even + odd, even)
     out[pl.ds(1, DEVICES, stride=3), :] = jnp.where(last, meta, odd)
     out[pl.ds(2, DEVICES, stride=3), :] = features[2].T
+    copy = pltpu.make_async_copy(out, out_hbm, w_sems.at[2])
+    copy.start()
+    copies.append(copy)
     for copy in copies:
         copy.wait()
 
@@ -582,15 +585,16 @@
                 terms.append(halves(e + f if n < 2 else e - f))
             v = [jnp.concatenate([t[h] for t in terms], axis=0) for h in range(2)]
             sides.append(dot3((tables[12 + parity], tables[14 + parity]), v))
+        spans = {15: [(0, 32, n)]} if n < 3 else {7: [(0, 8, 3), (24, 8, 4)], 15: [(8, 16, 5)]}
         for k in range(16):
             rows = slice(16 * k, 16 * k + 16)
             rows_out[k, :, cut] = sides[0][rows] + sides[1][rows]
             rows_out[31 - k, :, cut] = sides[0][rows] - sides[1][rows]
-        copy = pltpu.make_async_copy(
-            rows_out.at[:, :, pl.ds(256 * n, 256)], out.at[:, :, pl.ds(256 * n, 256)], sems.at[n]
-        )
-        copy.start()
-        copies.append(copy)
+            for at, size, sem in spans.get(k, ()):
+                place = (pl.ds(at, size), slice(None), pl.ds(256 * n, 256))
+                copy = pltpu.make_async_copy(rows_out.at[place], out.at[place], sems.at[sem])
+                copy.start()
+                copies.append(copy)
     for copy in copies:
         copy.wait()
 
@@ -618,12 +622,13 @@
     return pl.pallas_call(
         forward_kernel,
         in_specs=[SMEM] * 4 + [HBM] * 2 + [VMEM],
-        out_specs=[VMEM, HBM],
+        out_specs=[HBM, HBM],
         out_shape=[
             jax.ShapeDtypeStruct((768, 128), F32),
             jax.ShapeDtypeStruct((8, 256, 256), F32),
         ],
         scratch_shapes=[
+            pltpu.VMEM((768, 128), F32),
             pltpu.VMEM((BX, ROWS, NY), F32),
             pltpu.VMEM((2, 256, 256), BF16),
             pltpu.VMEM((2, 256, 256), BF16),
@@ -637,7 +642,7 @@
             pltpu.VMEM((3, 128, 256), F32),
             pltpu.SemaphoreType.DMA((2, 4)),
             pltpu.SemaphoreType.DMA((4,)),
-            pltpu.SemaphoreType.DMA((2,)),
+            pltpu.SemaphoreType.DMA((3,)),
         ],
         name="forward",
         **kw,
@@ -703,7 +708,7 @@
             pltpu.VMEM((3, 128, 256), F32),
             pltpu.VMEM((4, 512, 256), F32),
             pltpu.VMEM((BX, ROWS, NY), F32),
-            pltpu.SemaphoreType.DMA((4,)),
+            pltpu.SemaphoreType.DMA((6,)),
         ],
         compiler_params=GRANT,
         name="backward",

time: 70.7 us -> 70.3 us (level)
  no operation moved by 1% of the time
where the time goes in v4:
time: 70.3 us; the launch traced here: 70 us
  blocking collectives  23.8 us (34%)
  starting transfers between devices  15.7 us (22%)
  Pallas kernels  13.1 us (19%)
  waiting for transfers between devices  11 us (16%)
  local copies, waits for them, and re-layouts  5.72 us (8%)
  between operations  0.72 us (1%)
    all_to_all x1, blocking collectives, traded(): lax.all_to_all(pieces, ('mode', 'blk'), split_axis=0, concat_axis=0, tile...  23.8 us
    all_to_all x1, starting transfers between devices, traded(): lax.all_to_all(pieces, ('mode', 'blk'), split_axis=0, concat_axis=0, tile...  15.7 us
    all_to_all x1, waiting for transfers between devices, traded(): lax.all_to_all(pieces, ('mode', 'blk'), split_axis=0, concat_axis=0, tile...  11 us
    pallas_call x1, Pallas kernels, run_forward(): pl.pallas_call(forward_kernel, in_specs=[SMEM] * 4 + [HBM] * 2 + [VMEM],...  6.29 us
    unnamed x16, local copies, waits for them, and re-layouts  5.72 us
    pallas_call x1, Pallas kernels, run_backward(): pl.pallas_call(backward_kernel, in_specs=[SMEM] + [VMEM] * 4, out_specs=H...  3.37 us
    pallas_call x1, Pallas kernels, run_columns(): pl.pallas_call(column_kernel, in_specs=[VMEM] * 3, out_specs=VMEM, scratc...  3.03 us
  transfers between devices with their start and end apart: 1, of which 1 were waited for; matrix products, arithmetic and copies ran while one was open for 0% of the time, Pallas kernels for 1%

profile of v4, /device:TPU:1, one launch (start us, length us, event | category | flops | bytes accessed | tf_op | source)
XLA Modules:
  0.0 70.0 jit_solution(9471123019698139138)
XLA Ops:
  0.7 6.3 %forward.1 = (f32[768,128]{1,0:T(8,128)}, f32[8,256,256]{2,1,0:T(8,128)}) custom-call(s32[1]{0:T(128)S(6)} %copy.14.levels, s32[1,2]{1,0:T(1,128)} %neighbours.1, s32[3]{0:T(128)} %sweeps.1, s32[1]{0:T(128)} %bitcast.mode, f32[32,16,1024]{2,1,0:T(8,128)} %bitcast.11, bf16[16,256,256]{2,1,0:T(8,128)(2,1)} %constant.21.clone.tables_in.tables, ...), custom_call_target="tpu_custom_call" | custom-call | tf_op jit(solution)/shard_map/forward/pallas_call | solution.py:622
  6.9 15.7 %all-to-all-start = ((f32[256,1,384]{2,1,0:T(1,128)}), f32[256,1,384]{2,1,0:T(1,128)S(1)}, u32[]{:S(2)}, u32[]{:S(2)}) async-start(f32[256,1,384]{2,1,0:T(1,128)} %bitcast.12), calls=%async_computation | async-start | bytes 786432 | tf_op jit(solution)/shard_map/all_to_all | solution.py:721
  22.6 0.0 copy-start.3
  22.6 1.6 %copy-done.3 = f32[8,256,256]{2,1,0:T(8,128)S(1)} copy-done((f32[8,256,256]{2,1,0:T(8,128)S(1)}, f32[8,256,256]{2,1,0:T(8,128)}, u32[]{:S(2)}) %copy-start.3) | copy-done | bytes 2097176
  24.2 0.0 copy-start.4
  24.2 1.0 %copy-done.4 = f32[776,128]{1,0:T(8,128)S(1)} copy-done((f32[776,128]{1,0:T(8,128)S(1)}, f32[776,128]{1,0:T(8,128)}, u32[]{:S(2)}) %copy-start.4) | copy-done | bytes 397336
  25.2 0.0 copy-start.5
  25.2 0.9 %copy-done.5 = bf16[4,128,128]{2,1,0:T(8,128)(2,1)S(1)} copy-done((bf16[4,128,128]{2,1,0:T(8,128)(2,1)S(1)}, bf16[4,128,128]{2,1,0:T(8,128)(2,1)}, u32[]{:S(2)}) %copy-start.5) | copy-done | bytes 131096
  26.1 0.0 copy-start.6
  26.1 0.9 %copy-done.6 = f32[256,1,128]{2,1,0:T(1,128)S(1)} copy-done((f32[256,1,128]{2,1,0:T(1,128)S(1)}, f32[256,1,128]{2,1,0:T(1,128)}, u32[]{:S(2)}) %copy-start.6) | copy-done | bytes 131096
  27.0 0.0 copy-start
  27.0 0.0 copy-start.7
  27.0 0.4 prepare.1
  27.5 0.0 copy-start.1
  27.5 1.3 %copy-done.1 = f32[8,256,256]{2,1,0:T(8,128)} copy-done((f32[8,256,256]{2,1,0:T(8,128)}, f32[8,256,256]{2,1,0:T(8,128)S(1)}, u32[]{:S(2)}) %copy-start.1) | copy-done | bytes 2097176
  28.8 11.0 %all-to-all-done = f32[256,1,384]{2,1,0:T(1,128)S(1)} async-done(((f32[256,1,384]{2,1,0:T(1,128)}), f32[256,1,384]{2,1,0:T(1,128)S(1)}, u32[]{:S(2)}, u32[]{:S(2)}) %all-to-all-start) | async-done | bytes 393248 | tf_op jit(solution)/shard_map/all_to_all | solution.py:721
  39.8 0.0 copy-start.2
  39.8 3.0 %columns.1 = f32[768,128]{1,0:T(8,128)S(1)} custom-call(f32[768,128]{1,0:T(8,128)S(1)} %bitcast.8, f32[1048,128]{1,0:T(8,128)S(1)} %get-tuple-element.12.numbers, bf16[2048,128]{1,0:T(8,128)(2,1)S(1)} %get-tuple-element.13.terms_in), custom_call_target="tpu_custom_call" | custom-call | tf_op jit(solution)/shard_map/columns/pallas_call | solution.py:684
  42.8 23.8 %all_to_all.10 = f32[256,1,384]{2,1,0:T(1,128)S(1)} all-to-all(f32[256,1,384]{2,1,0:T(1,128)S(1)} %bitcast.10), channel_id=1, replica_groups=mesh['mode'=8,'blk'=32] {'mode','blk'}, dimensions={0} | all-to-all | bytes 786432 | tf_op jit(solution)/shard_map/all_to_all | solution.py:721
  66.6 0.0 copy-done
  66.6 0.0 copy-done.7
  66.6 0.0 copy-done.2
  66.6 3.4 %backward.1 = f32[32,16,1024]{2,1,0:T(8,128)} custom-call(s32[1]{0:T(128)S(6)} %copy.14.levels, f32[768,128]{1,0:T(8,128)S(1)} %bitcast.9, f32[8,256,256]{2,1,0:T(8,128)S(1)} %copy-done.2, bf16[16,256,256]{2,1,0:T(8,128)(2,1)S(1)} %copy-done, f32[1,1024]{1,0:T(1,128)S(1)} %copy-done.7), custom_call_target="tpu_custom_call" | custom-call | tf_op jit(solution)/shard_map/backward/pallas_call | solution.py:702
Async XLA Ops:
  6.9 32.8 %all-to-all-start = ((f32[256,1,384]{2,1,0:T(1,128)}), f32[256,1,384]{2,1,0:T(1,128)S(1)}, u32[]{:S(2)}, u32[]{:S(2)}) async-start(f32[256,1,384]{2,1,0:T(1,128)} %bitcast.12), calls=%async_computation | async-start | bytes 786432 | tf_op jit(solution)/shard_map/all_to_all | solution.py:721
  22.6 1.6 %copy-start.3 = (f32[8,256,256]{2,1,0:T(8,128)S(1)}, f32[8,256,256]{2,1,0:T(8,128)}, u32[]{:S(2)}) copy-start(f32[8,256,256]{2,1,0:T(8,128)} %get-tuple-element.11.w_in) | copy-start | bytes 6291460
  24.2 1.0 %copy-start.4 = (f32[776,128]{1,0:T(8,128)S(1)}, f32[776,128]{1,0:T(8,128)}, u32[]{:S(2)}) copy-start(f32[776,128]{1,0:T(8,128)} %constant.24.clone.constants_in) | copy-start | bytes 1191940
  25.2 0.9 %copy-start.5 = (bf16[4,128,128]{2,1,0:T(8,128)(2,1)S(1)}, bf16[4,128,128]{2,1,0:T(8,128)(2,1)}, u32[]{:S(2)}) copy-start(bf16[4,128,128]{2,1,0:T(8,128)(2,1)} %constant.25.clone.zbasis) | copy-start | bytes 393220
  26.1 0.9 %copy-start.6 = (f32[256,1,128]{2,1,0:T(1,128)S(1)}, f32[256,1,128]{2,1,0:T(1,128)}, u32[]{:S(2)}) copy-start(f32[256,1,128]{2,1,0:T(1,128)} %constant.23.clone.k_own) | copy-start | bytes 393220
  27.0 39.6 %copy-start = (bf16[16,256,256]{2,1,0:T(8,128)(2,1)S(1)}, bf16[16,256,256]{2,1,0:T(8,128)(2,1)}, u32[]{:S(2)}) copy-start(bf16[16,256,256]{2,1,0:T(8,128)(2,1)} %constant.21.clone.tables_in.tables) | copy-start | bytes 6291460
  27.0 39.6 %copy-start.7 = (f32[1,1024]{1,0:T(1,128)S(1)}, f32[1,1024]{1,0:T(1,128)}, u32[]{:S(2)}) copy-start(f32[1,1024]{1,0:T(1,128)} %constant.22.clone.kq) | copy-start | bytes 12292
  27.5 1.3 %copy-start.1 = (f32[8,256,256]{2,1,0:T(8,128)}, f32[8,256,256]{2,1,0:T(8,128)S(1)}, u32[]{:S(2)}) copy-start(f32[8,256,256]{2,1,0:T(8,128)S(1)} %get-tuple-element.14.w_in) | copy-start | bytes 6291460
  39.8 26.8 %copy-start.2 = (f32[8,256,256]{2,1,0:T(8,128)S(1)}, f32[8,256,256]{2,1,0:T(8,128)}, u32[]{:S(2)}) copy-start(f32[8,256,256]{2,1,0:T(8,128)} %copy-done.1) | copy-start | bytes 6291460

commit v5 on v4

--- a/solution.py
+++ b/solution.py
@@ -195,19 +195,23 @@
                     yh[q, rows, :] = high
                     yl[q, rows, :] = low
 
-    def transform(q):
-        for parity in range(2):
-            rows = slice(256 * parity, 256 * parity + 256)
-            f = dot3((yh[q, rows, :], yl[q, rows, :]), (t_h[q], t_l[q]))
-            high, low = halves(f)
-            fh[q, rows, :] = high
-            fl[q, rows, :] = low
+    def transform(unit):
+        q, parity = divmod(unit, 2)
+        rows = slice(256 * parity, 256 * parity + 256)
+        high, low = halves(dot3((yh[q, rows, :], yl[q, rows, :]), (t_h[q], t_l[q])))
+        fh[q, rows, :] = high
+        fl[q, rows, :] = low
+
+    def in_plane(unit):
+        q, parity = divmod(unit, 2)
+        rows = slice(256 * parity, 256 * parity + 256)
+        w_buffer[unit] = dot3((p_h[parity], p_l[parity]), (fh[q, rows, :], fl[q, rows, :]))
 
     for step in range(4):
         for copy in pieces_of(x, x_buffer, x_sems, step):
             copy.wait()
         if step == 3:
-            for copy in tables[:2]:
+            for copy in tables:
                 copy.wait()
         for k in range(4):
             fold(step, k)
@@ -237,37 +241,38 @@
             values = merged
         return values[0]
 
+    def divide(unit):
+        q, parity = divmod(unit, 2)
+        base = [column + kq[:, 256 * q : 256 * q + 256] for column in lambdas]
+        place = 32 * q + 16 * parity
+        totals = [None, None]
+        for group in range(2):
+            ends = [[], []]
+            for a in range(8 * group, 8 * group + 8):
+                shift = stiffness * np.float32(LX[IX[16 * parity + a]])
+                face = np.float32(SX[0, IX[16 * parity + a]])
+                for half in range(2):
+                    row = slice(16 * a + 8 * half, 16 * a + 8 * half + 8)
+                    w = w_buffer[unit, row, :] * inverted(base[half] + shift)
+                    w_buffer[unit, row, :] = w
+                    ends[half].append(w * firsts[half])
+                    part = face * w
+                    totals[half] = part if a == 0 else totals[half] + part
+            at = place + 8 * group
+            for half in range(2):
+                features[half, at : at + 8, :] = summed(ends[half])
+        for half in range(2):
+            features[2, place + 8 * half : place + 8 * half + 8, :] = totals[half]
+
     copies = []
     transform(0)
-    for copy in tables[2:]:
-        copy.wait()
-    for q in range(4):
-        if q < 3:
-            transform(q + 1)
-        base = [column + kq[:, 256 * q : 256 * q + 256] for column in lambdas]
-        for parity in range(2):
-            rows = slice(256 * parity, 256 * parity + 256)
-            g = dot3((p_h[parity], p_l[parity]), (fh[q, rows, :], fl[q, rows, :]))
-            place = 32 * q + 16 * parity
-            totals = [None, None]
-            for group in range(2):
-                ends = [[], []]
-                for a in range(8 * group, 8 * group + 8):
-                    shift = stiffness * np.float32(LX[IX[16 * parity + a]])
-                    face = np.float32(SX[0, IX[16 * parity + a]])
-                    for half in range(2):
-                        row = 16 * a + 8 * half
-                        w = g[row : row + 8] * inverted(base[half] + shift)
-                        w_buffer[2 * q + parity, row : row + 8, :] = w
-                        ends[half].append(w * firsts[half])
-                        part = face * w
-                        totals[half] = part if a == 0 else totals[half] + part
-                at = place + 8 * group
-                for half in range(2):
-                    features[half, at : at + 8, :] = summed(ends[half])
-            for half in range(2):
-                features[2, place + 8 * half : place + 8 * half + 8, :] = totals[half]
-        if q >= 2:
+    for unit in range(8):
+        if unit < 7:
+            transform(unit + 1)
+        in_plane(unit)
+        divide(unit)
+        q, parity = divmod(unit, 2)
+        if q >= 2 and parity == 1:
             span = pl.ds(0, 6) if q == 2 else pl.ds(6, 2)
             copy = pltpu.make_async_copy(w_buffer.at[span], w_out.at[span], w_sems.at[q - 2])
             copy.start()
@@ -350,7 +355,7 @@
     links = (terms_in[0:768], terms_in[768:1536])
     zsum = numbers[Z_SUM : Z_SUM + 128]
     zbasis = [terms_in[1536 + 128 * n : 1536 + 128 * n + 128] for n in range(4)]
-    meta = inbox[pl.ds(96 * (BLOCKS - 1) + 1, 32, stride=3), :]
+    meta = inbox[pl.ds(3 * (BLOCKS - 1) + 1, 32, stride=24), :]
     stiff_col = meta[:, 0:1]
     flat = stiff_col < 2.0
     middle = stiff_col < 8.0
@@ -423,7 +428,7 @@
         return sides
 
     def received(kind, m):
-        return inbox[pl.ds(96 * m + kind, 32, stride=3), :]
+        return inbox[pl.ds(3 * m + kind, 32, stride=24), :]
 
     even = [received(0, m) for m in range(BLOCKS)]
     odd = [received(1, m) for m in range(BLOCKS - 1)] + [jnp.zeros((32, 128), F32)]
@@ -527,7 +532,7 @@
                 )
     faces = turned[...].T
     for m in range(BLOCKS):
-        out[pl.ds(96 * m + 2, 32, stride=3), :] = faces[32 * m : 32 * m + 32]
+        out[pl.ds(3 * m + 2, 32, stride=24), :] = faces[32 * m : 32 * m + 32]
     levelled = [
         jnp.concatenate([link[256 * n : 256 * n + 256, :] for n in range(3)], axis=1)
         for link in links
@@ -539,7 +544,7 @@
     )
     for m in range(BLOCKS):
         for kind in range(2):
-            out[pl.ds(96 * m + kind, 32, stride=3), :] = sides[m][kind]
+            out[pl.ds(3 * m + kind, 32, stride=24), :] = sides[m][kind]
 
 
 def backward_kernel(
@@ -718,13 +723,13 @@
 
 def traded(outbox):
     pieces = outbox.reshape(DEVICES, 1, 384)
-    pieces = lax.all_to_all(pieces, ("mode", "blk"), split_axis=0, concat_axis=0, tiled=True)
+    pieces = lax.all_to_all(pieces, ("blk", "mode"), split_axis=0, concat_axis=0, tiled=True)
     return pieces.reshape(3 * DEVICES, 128)
 
 
 def body(divergence, neighbours, levels, sweeps):
     mode = lax.axis_index("mode").astype(jnp.int32)
-    device = mode * 32 + lax.axis_index("blk").astype(jnp.int32)
+    device = lax.axis_index("blk").astype(jnp.int32) * BLOCKS + mode
     outbox, w = run_forward(levels, neighbours, sweeps, mode[None], divergence[0])
     numbers, terms, w = run_prepare(device[None], w)
     outbox = run_columns(traded(outbox), numbers, terms)

time: 70.3 us -> 69.3 us (0.986)
  no operation moved by 1% of the time
where the time goes in v5:
time: 69.3 us; the launch traced here: 69 us
  blocking collectives  23.2 us (33%)
  starting transfers between devices  15.7 us (23%)
  Pallas kernels  12.8 us (18%)
  waiting for transfers between devices  10.9 us (16%)
  local copies, waits for them, and re-layouts  5.72 us (8%)
  between operations  0.72 us (1%)
    all_to_all x1, blocking collectives, traded(): lax.all_to_all(pieces, ('blk', 'mode'), split_axis=0, concat_axis=0, tile...  23.2 us
    all_to_all x1, starting transfers between devices, traded(): lax.all_to_all(pieces, ('blk', 'mode'), split_axis=0, concat_axis=0, tile...  15.7 us
    all_to_all x1, waiting for transfers between devices, traded(): lax.all_to_all(pieces, ('blk', 'mode'), split_axis=0, concat_axis=0, tile...  10.9 us
    pallas_call x1, Pallas kernels, run_forward(): pl.pallas_call(forward_kernel, in_specs=[SMEM] * 4 + [HBM] * 2 + [VMEM],...  6.01 us
    unnamed x16, local copies, waits for them, and re-layouts  5.72 us
    pallas_call x1, Pallas kernels, run_backward(): pl.pallas_call(backward_kernel, in_specs=[SMEM] + [VMEM] * 4, out_specs=H...  3.37 us
    pallas_call x1, Pallas kernels, run_columns(): pl.pallas_call(column_kernel, in_specs=[VMEM] * 3, out_specs=VMEM, scratc...  3.03 us
  transfers between devices with their start and end apart: 1, of which 1 were waited for; matrix products, arithmetic and copies ran while one was open for 0% of the time, Pallas kernels for 1%

profile of v5, /device:TPU:1, one launch (start us, length us, event | category | flops | bytes accessed | tf_op | source)
XLA Modules:
  0.0 69.0 jit_solution(5758773518904457128)
XLA Ops:
  0.7 6.0 %forward.1 = (f32[768,128]{1,0:T(8,128)}, f32[8,256,256]{2,1,0:T(8,128)}) custom-call(s32[1]{0:T(128)S(6)} %copy.14.levels, s32[1,2]{1,0:T(1,128)} %neighbours.1, s32[3]{0:T(128)} %sweeps.1, s32[1]{0:T(128)} %bitcast.mode, f32[32,16,1024]{2,1,0:T(8,128)} %bitcast.11, bf16[16,256,256]{2,1,0:T(8,128)(2,1)} %constant.21.clone.tables_in.tables, ...), custom_call_target="tpu_custom_call" | custom-call | tf_op jit(solution)/shard_map/forward/pallas_call | solution.py:627
  6.7 15.7 %all-to-all-start = ((f32[256,1,384]{2,1,0:T(1,128)}), f32[256,1,384]{2,1,0:T(1,128)S(1)}, u32[]{:S(2)}, u32[]{:S(2)}) async-start(f32[256,1,384]{2,1,0:T(1,128)} %bitcast.12), calls=%async_computation | async-start | bytes 786432 | tf_op jit(solution)/shard_map/all_to_all | solution.py:726
  22.3 0.0 copy-start.3
  22.3 1.6 %copy-done.3 = f32[8,256,256]{2,1,0:T(8,128)S(1)} copy-done((f32[8,256,256]{2,1,0:T(8,128)S(1)}, f32[8,256,256]{2,1,0:T(8,128)}, u32[]{:S(2)}) %copy-start.3) | copy-done | bytes 2097176
  23.9 0.0 copy-start.4
  23.9 1.0 %copy-done.4 = f32[776,128]{1,0:T(8,128)S(1)} copy-done((f32[776,128]{1,0:T(8,128)S(1)}, f32[776,128]{1,0:T(8,128)}, u32[]{:S(2)}) %copy-start.4) | copy-done | bytes 397336
  24.9 0.0 copy-start.5
  24.9 0.9 %copy-done.5 = bf16[4,128,128]{2,1,0:T(8,128)(2,1)S(1)} copy-done((bf16[4,128,128]{2,1,0:T(8,128)(2,1)S(1)}, bf16[4,128,128]{2,1,0:T(8,128)(2,1)}, u32[]{:S(2)}) %copy-start.5) | copy-done | bytes 131096
  25.8 0.0 copy-start.6
  25.8 0.9 %copy-done.6 = f32[256,1,128]{2,1,0:T(1,128)S(1)} copy-done((f32[256,1,128]{2,1,0:T(1,128)S(1)}, f32[256,1,128]{2,1,0:T(1,128)}, u32[]{:S(2)}) %copy-start.6) | copy-done | bytes 131096
  26.7 0.0 copy-start
  26.7 0.0 copy-start.7
  26.7 0.4 prepare.1
  27.2 0.0 copy-start.1
  27.2 1.3 %copy-done.1 = f32[8,256,256]{2,1,0:T(8,128)} copy-done((f32[8,256,256]{2,1,0:T(8,128)}, f32[8,256,256]{2,1,0:T(8,128)S(1)}, u32[]{:S(2)}) %copy-start.1) | copy-done | bytes 2097176
  28.5 10.9 %all-to-all-done = f32[256,1,384]{2,1,0:T(1,128)S(1)} async-done(((f32[256,1,384]{2,1,0:T(1,128)}), f32[256,1,384]{2,1,0:T(1,128)S(1)}, u32[]{:S(2)}, u32[]{:S(2)}) %all-to-all-start) | async-done | bytes 393248 | tf_op jit(solution)/shard_map/all_to_all | solution.py:726
  39.4 0.0 copy-start.2
  39.4 3.0 %columns.1 = f32[768,128]{1,0:T(8,128)S(1)} custom-call(f32[768,128]{1,0:T(8,128)S(1)} %bitcast.8, f32[1048,128]{1,0:T(8,128)S(1)} %get-tuple-element.12.numbers, bf16[2048,128]{1,0:T(8,128)(2,1)S(1)} %get-tuple-element.13.terms_in), custom_call_target="tpu_custom_call" | custom-call | tf_op jit(solution)/shard_map/columns/pallas_call | solution.py:689
  42.5 23.2 %all_to_all.10 = f32[256,1,384]{2,1,0:T(1,128)S(1)} all-to-all(f32[256,1,384]{2,1,0:T(1,128)S(1)} %bitcast.10), channel_id=1, replica_groups=mesh['mode'=8,'blk'=32] {'blk','mode'}, dimensions={0} | all-to-all | bytes 786432 | tf_op jit(solution)/shard_map/all_to_all | solution.py:726
  65.6 0.0 copy-done
  65.6 0.0 copy-done.7
  65.6 0.0 copy-done.2
  65.6 3.4 %backward.1 = f32[32,16,1024]{2,1,0:T(8,128)} custom-call(s32[1]{0:T(128)S(6)} %copy.14.levels, f32[768,128]{1,0:T(8,128)S(1)} %bitcast.9, f32[8,256,256]{2,1,0:T(8,128)S(1)} %copy-done.2, bf16[16,256,256]{2,1,0:T(8,128)(2,1)S(1)} %copy-done, f32[1,1024]{1,0:T(1,128)S(1)} %copy-done.7), custom_call_target="tpu_custom_call" | custom-call | tf_op jit(solution)/shard_map/backward/pallas_call | solution.py:707
Async XLA Ops:
  6.7 32.8 %all-to-all-start = ((f32[256,1,384]{2,1,0:T(1,128)}), f32[256,1,384]{2,1,0:T(1,128)S(1)}, u32[]{:S(2)}, u32[]{:S(2)}) async-start(f32[256,1,384]{2,1,0:T(1,128)} %bitcast.12), calls=%async_computation | async-start | bytes 786432 | tf_op jit(solution)/shard_map/all_to_all | solution.py:726
  22.3 1.6 %copy-start.3 = (f32[8,256,256]{2,1,0:T(8,128)S(1)}, f32[8,256,256]{2,1,0:T(8,128)}, u32[]{:S(2)}) copy-start(f32[8,256,256]{2,1,0:T(8,128)} %get-tuple-element.11.w_in) | copy-start | bytes 6291460
  23.9 1.0 %copy-start.4 = (f32[776,128]{1,0:T(8,128)S(1)}, f32[776,128]{1,0:T(8,128)}, u32[]{:S(2)}) copy-start(f32[776,128]{1,0:T(8,128)} %constant.24.clone.constants_in) | copy-start | bytes 1191940
  24.9 0.9 %copy-start.5 = (bf16[4,128,128]{2,1,0:T(8,128)(2,1)S(1)}, bf16[4,128,128]{2,1,0:T(8,128)(2,1)}, u32[]{:S(2)}) copy-start(bf16[4,128,128]{2,1,0:T(8,128)(2,1)} %constant.25.clone.zbasis) | copy-start | bytes 393220
  25.8 0.9 %copy-start.6 = (f32[256,1,128]{2,1,0:T(1,128)S(1)}, f32[256,1,128]{2,1,0:T(1,128)}, u32[]{:S(2)}) copy-start(f32[256,1,128]{2,1,0:T(1,128)} %constant.23.clone.k_own) | copy-start | bytes 393220
  26.7 38.9 %copy-start = (bf16[16,256,256]{2,1,0:T(8,128)(2,1)S(1)}, bf16[16,256,256]{2,1,0:T(8,128)(2,1)}, u32[]{:S(2)}) copy-start(bf16[16,256,256]{2,1,0:T(8,128)(2,1)} %constant.21.clone.tables_in.tables) | copy-start | bytes 6291460
  26.7 38.9 %copy-start.7 = (f32[1,1024]{1,0:T(1,128)S(1)}, f32[1,1024]{1,0:T(1,128)}, u32[]{:S(2)}) copy-start(f32[1,1024]{1,0:T(1,128)} %constant.22.clone.kq) | copy-start | bytes 12292
  27.2 1.3 %copy-start.1 = (f32[8,256,256]{2,1,0:T(8,128)}, f32[8,256,256]{2,1,0:T(8,128)S(1)}, u32[]{:S(2)}) copy-start(f32[8,256,256]{2,1,0:T(8,128)S(1)} %get-tuple-element.14.w_in) | copy-start | bytes 6291460
  39.4 26.2 %copy-start.2 = (f32[8,256,256]{2,1,0:T(8,128)S(1)}, f32[8,256,256]{2,1,0:T(8,128)}, u32[]{:S(2)}) copy-start(f32[8,256,256]{2,1,0:T(8,128)} %copy-done.1) | copy-start | bytes 6291460

commit v6 on v5

--- a/solution.py
+++ b/solution.py
@@ -156,19 +156,21 @@
     out_hbm, w_out, out, x_buffer, p_h, p_l, t_h, t_l, yh, yl, fh, fl, w_buffer, features,
     x_sems, t_sems, w_sems,
 ):
-    tables = [
-        pltpu.make_async_copy(source, place, t_sems.at[n])
-        for n, (source, place) in enumerate(
-            (
-                (tables_in.at[pl.ds(0, 4)], t_h), (tables_in.at[pl.ds(4, 4)], t_l),
-                (tables_in.at[pl.ds(8, 2)], p_h), (tables_in.at[pl.ds(10, 2)], p_l),
-            )
-        )
+    planes = [
+        pltpu.make_async_copy(tables_in.at[pl.ds(8 + 2 * n, 2)], place, t_sems.at[8 + n])
+        for n, place in enumerate((p_h, p_l))
+    ]
+    classes = [
+        [
+            pltpu.make_async_copy(tables_in.at[4 * n + q], place.at[q], t_sems.at[2 * q + n])
+            for n, place in enumerate((t_h, t_l))
+        ]
+        for q in range(4)
     ]
     for step in range(4):
         for copy in pieces_of(x, x_buffer, x_sems, step):
             copy.start()
-    for copy in tables:
+    for copy in classes[0] + planes + classes[1] + classes[2] + classes[3]:
         copy.start()
 
     def fold(step, k):
@@ -211,7 +213,7 @@
         for copy in pieces_of(x, x_buffer, x_sems, step):
             copy.wait()
         if step == 3:
-            for copy in tables:
+            for copy in classes[0]:
                 copy.wait()
         for k in range(4):
             fold(step, k)
@@ -269,6 +271,9 @@
     for unit in range(8):
         if unit < 7:
             transform(unit + 1)
+        if unit == 0:
+            for copy in planes + classes[1] + classes[2] + classes[3]:
+                copy.wait()
         in_plane(unit)
         divide(unit)
         q, parity = divmod(unit, 2)
@@ -646,7 +651,7 @@
             pltpu.VMEM((8, 256, 256), F32),
             pltpu.VMEM((3, 128, 256), F32),
             pltpu.SemaphoreType.DMA((2, 4)),
-            pltpu.SemaphoreType.DMA((4,)),
+            pltpu.SemaphoreType.DMA((10,)),
             pltpu.SemaphoreType.DMA((3,)),
         ],
         name="forward",

time: 69.3 us -> 69.5 us (level)
  no operation moved by 1% of the time
where the time goes in v6:
time: 69.5 us; the launch traced here: 69.2 us
  blocking collectives  23.2 us (33%)
  starting transfers between devices  15.7 us (23%)
  Pallas kernels  13 us (19%)
  waiting for transfers between devices  10.9 us (16%)
  local copies, waits for them, and re-layouts  5.72 us (8%)
  between operations  0.72 us (1%)
    all_to_all x1, blocking collectives, traded(): lax.all_to_all(pieces, ('blk', 'mode'), split_axis=0, concat_axis=0, tile...  23.2 us
    all_to_all x1, starting transfers between devices, traded(): lax.all_to_all(pieces, ('blk', 'mode'), split_axis=0, concat_axis=0, tile...  15.7 us
    all_to_all x1, waiting for transfers between devices, traded(): lax.all_to_all(pieces, ('blk', 'mode'), split_axis=0, concat_axis=0, tile...  10.9 us
    pallas_call x1, Pallas kernels, run_forward(): pl.pallas_call(forward_kernel, in_specs=[SMEM] * 4 + [HBM] * 2 + [VMEM],...  6.18 us
    unnamed x16, local copies, waits for them, and re-layouts  5.72 us
    pallas_call x1, Pallas kernels, run_backward(): pl.pallas_call(backward_kernel, in_specs=[SMEM] + [VMEM] * 4, out_specs=H...  3.37 us
    pallas_call x1, Pallas kernels, run_columns(): pl.pallas_call(column_kernel, in_specs=[VMEM] * 3, out_specs=VMEM, scratc...  3.04 us
  transfers between devices with their start and end apart: 1, of which 1 were waited for; matrix products, arithmetic and copies ran while one was open for 0% of the time, Pallas kernels for 1%

profile of v6, /device:TPU:1, one launch (start us, length us, event | category | flops | bytes accessed | tf_op | source)
XLA Modules:
  0.0 69.2 jit_solution(6493247473254178529)
XLA Ops:
  0.7 6.2 %forward.1 = (f32[768,128]{1,0:T(8,128)}, f32[8,256,256]{2,1,0:T(8,128)}) custom-call(s32[1]{0:T(128)S(6)} %copy.14.levels, s32[1,2]{1,0:T(1,128)} %neighbours.1, s32[3]{0:T(128)} %sweeps.1, s32[1]{0:T(128)} %bitcast.mode, f32[32,16,1024]{2,1,0:T(8,128)} %bitcast.11, bf16[16,256,256]{2,1,0:T(8,128)(2,1)} %constant.21.clone.tables_in.tables, ...), custom_call_target="tpu_custom_call" | custom-call | tf_op jit(solution)/shard_map/forward/pallas_call | solution.py:632
  6.8 15.7 %all-to-all-start = ((f32[256,1,384]{2,1,0:T(1,128)}), f32[256,1,384]{2,1,0:T(1,128)S(1)}, u32[]{:S(2)}, u32[]{:S(2)}) async-start(f32[256,1,384]{2,1,0:T(1,128)} %bitcast.12), calls=%async_computation | async-start | bytes 786432 | tf_op jit(solution)/shard_map/all_to_all | solution.py:731
  22.5 0.0 copy-start.3
  22.5 1.6 %copy-done.3 = f32[8,256,256]{2,1,0:T(8,128)S(1)} copy-done((f32[8,256,256]{2,1,0:T(8,128)S(1)}, f32[8,256,256]{2,1,0:T(8,128)}, u32[]{:S(2)}) %copy-start.3) | copy-done | bytes 2097176
  24.1 0.0 copy-start.4
  24.1 1.0 %copy-done.4 = f32[776,128]{1,0:T(8,128)S(1)} copy-done((f32[776,128]{1,0:T(8,128)S(1)}, f32[776,128]{1,0:T(8,128)}, u32[]{:S(2)}) %copy-start.4) | copy-done | bytes 397336
  25.1 0.0 copy-start.5
  25.1 0.9 %copy-done.5 = bf16[4,128,128]{2,1,0:T(8,128)(2,1)S(1)} copy-done((bf16[4,128,128]{2,1,0:T(8,128)(2,1)S(1)}, bf16[4,128,128]{2,1,0:T(8,128)(2,1)}, u32[]{:S(2)}) %copy-start.5) | copy-done | bytes 131096
  26.0 0.0 copy-start.6
  26.0 0.9 %copy-done.6 = f32[256,1,128]{2,1,0:T(1,128)S(1)} copy-done((f32[256,1,128]{2,1,0:T(1,128)S(1)}, f32[256,1,128]{2,1,0:T(1,128)}, u32[]{:S(2)}) %copy-start.6) | copy-done | bytes 131096
  26.9 0.0 copy-start
  26.9 0.0 copy-start.7
  26.9 0.4 prepare.1
  27.4 0.0 copy-start.1
  27.4 1.3 %copy-done.1 = f32[8,256,256]{2,1,0:T(8,128)} copy-done((f32[8,256,256]{2,1,0:T(8,128)}, f32[8,256,256]{2,1,0:T(8,128)S(1)}, u32[]{:S(2)}) %copy-start.1) | copy-done | bytes 2097176
  28.7 10.9 %all-to-all-done = f32[256,1,384]{2,1,0:T(1,128)S(1)} async-done(((f32[256,1,384]{2,1,0:T(1,128)}), f32[256,1,384]{2,1,0:T(1,128)S(1)}, u32[]{:S(2)}, u32[]{:S(2)}) %all-to-all-start) | async-done | bytes 393248 | tf_op jit(solution)/shard_map/all_to_all | solution.py:731
  39.6 0.0 copy-start.2
  39.6 3.0 %columns.1 = f32[768,128]{1,0:T(8,128)S(1)} custom-call(f32[768,128]{1,0:T(8,128)S(1)} %bitcast.8, f32[1048,128]{1,0:T(8,128)S(1)} %get-tuple-element.12.numbers, bf16[2048,128]{1,0:T(8,128)(2,1)S(1)} %get-tuple-element.13.terms_in), custom_call_target="tpu_custom_call" | custom-call | tf_op jit(solution)/shard_map/columns/pallas_call | solution.py:694
  42.6 23.2 %all_to_all.10 = f32[256,1,384]{2,1,0:T(1,128)S(1)} all-to-all(f32[256,1,384]{2,1,0:T(1,128)S(1)} %bitcast.10), channel_id=1, replica_groups=mesh['mode'=8,'blk'=32] {'blk','mode'}, dimensions={0} | all-to-all | bytes 786432 | tf_op jit(solution)/shard_map/all_to_all | solution.py:731
  65.8 0.0 copy-done
  65.8 0.0 copy-done.7
  65.8 0.0 copy-done.2
  65.8 3.4 %backward.1 = f32[32,16,1024]{2,1,0:T(8,128)} custom-call(s32[1]{0:T(128)S(6)} %copy.14.levels, f32[768,128]{1,0:T(8,128)S(1)} %bitcast.9, f32[8,256,256]{2,1,0:T(8,128)S(1)} %copy-done.2, bf16[16,256,256]{2,1,0:T(8,128)(2,1)S(1)} %copy-done, f32[1,1024]{1,0:T(1,128)S(1)} %copy-done.7), custom_call_target="tpu_custom_call" | custom-call | tf_op jit(solution)/shard_map/backward/pallas_call | solution.py:712
Async XLA Ops:
  6.8 32.8 %all-to-all-start = ((f32[256,1,384]{2,1,0:T(1,128)}), f32[256,1,384]{2,1,0:T(1,128)S(1)}, u32[]{:S(2)}, u32[]{:S(2)}) async-start(f32[256,1,384]{2,1,0:T(1,128)} %bitcast.12), calls=%async_computation | async-start | bytes 786432 | tf_op jit(solution)/shard_map/all_to_all | solution.py:731
  22.5 1.6 %copy-start.3 = (f32[8,256,256]{2,1,0:T(8,128)S(1)}, f32[8,256,256]{2,1,0:T(8,128)}, u32[]{:S(2)}) copy-start(f32[8,256,256]{2,1,0:T(8,128)} %get-tuple-element.11.w_in) | copy-start | bytes 6291460
  24.1 1.0 %copy-start.4 = (f32[776,128]{1,0:T(8,128)S(1)}, f32[776,128]{1,0:T(8,128)}, u32[]{:S(2)}) copy-start(f32[776,128]{1,0:T(8,128)} %constant.24.clone.constants_in) | copy-start | bytes 1191940
  25.1 0.9 %copy-start.5 = (bf16[4,128,128]{2,1,0:T(8,128)(2,1)S(1)}, bf16[4,128,128]{2,1,0:T(8,128)(2,1)}, u32[]{:S(2)}) copy-start(bf16[4,128,128]{2,1,0:T(8,128)(2,1)} %constant.25.clone.zbasis) | copy-start | bytes 393220
  26.0 0.9 %copy-start.6 = (f32[256,1,128]{2,1,0:T(1,128)S(1)}, f32[256,1,128]{2,1,0:T(1,128)}, u32[]{:S(2)}) copy-start(f32[256,1,128]{2,1,0:T(1,128)} %constant.23.clone.k_own) | copy-start | bytes 393220
  26.9 38.9 %copy-start = (bf16[16,256,256]{2,1,0:T(8,128)(2,1)S(1)}, bf16[16,256,256]{2,1,0:T(8,128)(2,1)}, u32[]{:S(2)}) copy-start(bf16[16,256,256]{2,1,0:T(8,128)(2,1)} %constant.21.clone.tables_in.tables) | copy-start | bytes 6291460
  26.9 38.9 %copy-start.7 = (f32[1,1024]{1,0:T(1,128)S(1)}, f32[1,1024]{1,0:T(1,128)}, u32[]{:S(2)}) copy-start(f32[1,1024]{1,0:T(1,128)} %constant.22.clone.kq) | copy-start | bytes 12292
  27.4 1.3 %copy-start.1 = (f32[8,256,256]{2,1,0:T(8,128)}, f32[8,256,256]{2,1,0:T(8,128)S(1)}, u32[]{:S(2)}) copy-start(f32[8,256,256]{2,1,0:T(8,128)S(1)} %get-tuple-element.14.w_in) | copy-start | bytes 6291460
  39.6 26.2 %copy-start.2 = (f32[8,256,256]{2,1,0:T(8,128)S(1)}, f32[8,256,256]{2,1,0:T(8,128)}, u32[]{:S(2)}) copy-start(f32[8,256,256]{2,1,0:T(8,128)} %copy-done.1) | copy-start | bytes 6291460

commit v7 on v5

--- a/solution.py
+++ b/solution.py
@@ -144,9 +144,9 @@
 
 
 def pieces_of(x, x_buffer, x_sems, step):
-    first, second = 4 * step, 28 - 4 * step
+    first, second = 2 * step, 30 - 2 * step
     return [
-        pltpu.make_async_copy(x.at[pl.ds(at, 4)], x_buffer.at[pl.ds(at, 4)], x_sems.at[n, step])
+        pltpu.make_async_copy(x.at[pl.ds(at, 2)], x_buffer.at[pl.ds(at, 2)], x_sems.at[n, step])
         for n, at in enumerate((first, second))
     ]
 
@@ -165,7 +165,7 @@
             )
         )
     ]
-    for step in range(4):
+    for step in range(8):
         for copy in pieces_of(x, x_buffer, x_sems, step):
             copy.start()
     for copy in tables:
@@ -174,7 +174,7 @@
     def fold(step, k):
         for parity in range(2):
             for k in (k,):
-                a, b = x_buffer[4 * step + k], x_buffer[31 - 4 * step - k]
+                a, b = x_buffer[2 * step + k], x_buffer[31 - 2 * step - k]
                 v = a + b if parity == 0 else a - b
                 v0, v1, v2, v3 = (v[:, 256 * n : 256 * n + 256] for n in range(4))
                 e0, e1 = v0 + v2, v1 + v3
@@ -188,7 +188,7 @@
                     jnp.concatenate((f0 + turn0, g0 + turn1), axis=1),
                     jnp.concatenate((f0 - turn0, g0 - turn1), axis=1),
                 )
-                at = 256 * parity + 16 * (4 * step + k)
+                at = 256 * parity + 16 * (2 * step + k)
                 rows = slice(at, at + 16)
                 for q in range(4):
                     high, low = halves(parts[q])
@@ -207,13 +207,13 @@
         rows = slice(256 * parity, 256 * parity + 256)
         w_buffer[unit] = dot3((p_h[parity], p_l[parity]), (fh[q, rows, :], fl[q, rows, :]))
 
-    for step in range(4):
+    for step in range(8):
         for copy in pieces_of(x, x_buffer, x_sems, step):
             copy.wait()
-        if step == 3:
+        if step == 7:
             for copy in tables:
                 copy.wait()
-        for k in range(4):
+        for k in range(2):
             fold(step, k)
     level = levels[0]
     stiffness = stiffness_scalar(level)
@@ -289,13 +289,17 @@
     for n, fact in enumerate(facts):
         meta = jnp.where(lane == n, fact, meta)
     meta = jnp.concatenate([meta] * (DEVICES // 8), axis=0)
-    even, odd = features[0].T, features[1].T
-    out[pl.ds(0, DEVICES, stride=3), :] = jnp.where(last, even + odd, even)
-    out[pl.ds(1, DEVICES, stride=3), :] = jnp.where(last, meta, odd)
-    out[pl.ds(2, DEVICES, stride=3), :] = features[2].T
-    copy = pltpu.make_async_copy(out, out_hbm, w_sems.at[2])
-    copy.start()
-    copies.append(copy)
+    for part in range(2):
+        cut = slice(128 * part, 128 * part + 128)
+        even, odd, sides = (features[kind, :, cut].T for kind in range(3))
+        first = 384 * part
+        out[pl.ds(first, 128, stride=3), :] = jnp.where(last, even + odd, even)
+        out[pl.ds(first + 1, 128, stride=3), :] = jnp.where(last, meta[cut], odd)
+        out[pl.ds(first + 2, 128, stride=3), :] = sides
+        span = pl.ds(first, 384)
+        copy = pltpu.make_async_copy(out.at[span], out_hbm.at[span], w_sems.at[2 + part])
+        copy.start()
+        copies.append(copy)
     for copy in copies:
         copy.wait()
 
@@ -645,9 +649,9 @@
             pltpu.VMEM((4, 512, 256), BF16),
             pltpu.VMEM((8, 256, 256), F32),
             pltpu.VMEM((3, 128, 256), F32),
-            pltpu.SemaphoreType.DMA((2, 4)),
+            pltpu.SemaphoreType.DMA((2, 8)),
             pltpu.SemaphoreType.DMA((4,)),
-            pltpu.SemaphoreType.DMA((3,)),
+            pltpu.SemaphoreType.DMA((4,)),
         ],
         name="forward",
         **kw,

time: 69.3 us -> 69.5 us (level)
  no operation moved by 1% of the time
where the time goes in v7:
time: 69.5 us; the launch traced here: 69.2 us
  blocking collectives  23.2 us (33%)
  starting transfers between devices  15.7 us (23%)
  Pallas kernels  13 us (19%)
  waiting for transfers between devices  10.9 us (16%)
  local copies, waits for them, and re-layouts  5.72 us (8%)
  between operations  0.72 us (1%)
    all_to_all x1, blocking collectives, traded(): lax.all_to_all(pieces, ('blk', 'mode'), split_axis=0, concat_axis=0, tile...  23.2 us
    all_to_all x1, starting transfers between devices, traded(): lax.all_to_all(pieces, ('blk', 'mode'), split_axis=0, concat_axis=0, tile...  15.7 us
    all_to_all x1, waiting for transfers between devices, traded(): lax.all_to_all(pieces, ('blk', 'mode'), split_axis=0, concat_axis=0, tile...  10.9 us
    pallas_call x1, Pallas kernels, run_forward(): pl.pallas_call(forward_kernel, in_specs=[SMEM] * 4 + [HBM] * 2 + [VMEM],...  6.18 us
    unnamed x16, local copies, waits for them, and re-layouts  5.72 us
    pallas_call x1, Pallas kernels, run_backward(): pl.pallas_call(backward_kernel, in_specs=[SMEM] + [VMEM] * 4, out_specs=H...  3.37 us
    pallas_call x1, Pallas kernels, run_columns(): pl.pallas_call(column_kernel, in_specs=[VMEM] * 3, out_specs=VMEM, scratc...  3.04 us
  transfers between devices with their start and end apart: 1, of which 1 were waited for; matrix products, arithmetic and copies ran while one was open for 0% of the time, Pallas kernels for 1%

profile of v7, /device:TPU:1, one launch (start us, length us, event | category | flops | bytes accessed | tf_op | source)
XLA Modules:
  0.0 69.2 jit_solution(11320541331496077311)
XLA Ops:
  0.7 6.2 %forward.1 = (f32[768,128]{1,0:T(8,128)}, f32[8,256,256]{2,1,0:T(8,128)}) custom-call(s32[1]{0:T(128)S(6)} %copy.14.levels, s32[1,2]{1,0:T(1,128)} %neighbours.1, s32[3]{0:T(128)} %sweeps.1, s32[1]{0:T(128)} %bitcast.mode, f32[32,16,1024]{2,1,0:T(8,128)} %bitcast.11, bf16[16,256,256]{2,1,0:T(8,128)(2,1)} %constant.21.clone.tables_in.tables, ...), custom_call_target="tpu_custom_call" | custom-call | tf_op jit(solution)/shard_map/forward/pallas_call | solution.py:631
  6.8 15.7 %all-to-all-start = ((f32[256,1,384]{2,1,0:T(1,128)}), f32[256,1,384]{2,1,0:T(1,128)S(1)}, u32[]{:S(2)}, u32[]{:S(2)}) async-start(f32[256,1,384]{2,1,0:T(1,128)} %bitcast.12), calls=%async_computation | async-start | bytes 786432 | tf_op jit(solution)/shard_map/all_to_all | solution.py:730
  22.5 0.0 copy-start.3
  22.5 1.6 %copy-done.3 = f32[8,256,256]{2,1,0:T(8,128)S(1)} copy-done((f32[8,256,256]{2,1,0:T(8,128)S(1)}, f32[8,256,256]{2,1,0:T(8,128)}, u32[]{:S(2)}) %copy-start.3) | copy-done | bytes 2097176
  24.1 0.0 copy-start.4
  24.1 1.0 %copy-done.4 = f32[776,128]{1,0:T(8,128)S(1)} copy-done((f32[776,128]{1,0:T(8,128)S(1)}, f32[776,128]{1,0:T(8,128)}, u32[]{:S(2)}) %copy-start.4) | copy-done | bytes 397336
  25.1 0.0 copy-start.5
  25.1 0.9 %copy-done.5 = bf16[4,128,128]{2,1,0:T(8,128)(2,1)S(1)} copy-done((bf16[4,128,128]{2,1,0:T(8,128)(2,1)S(1)}, bf16[4,128,128]{2,1,0:T(8,128)(2,1)}, u32[]{:S(2)}) %copy-start.5) | copy-done | bytes 131096
  26.0 0.0 copy-start.6
  26.0 0.9 %copy-done.6 = f32[256,1,128]{2,1,0:T(1,128)S(1)} copy-done((f32[256,1,128]{2,1,0:T(1,128)S(1)}, f32[256,1,128]{2,1,0:T(1,128)}, u32[]{:S(2)}) %copy-start.6) | copy-done | bytes 131096
  26.9 0.0 copy-start
  26.9 0.0 copy-start.7
  26.9 0.4 prepare.1
  27.4 0.0 copy-start.1
  27.4 1.3 %copy-done.1 = f32[8,256,256]{2,1,0:T(8,128)} copy-done((f32[8,256,256]{2,1,0:T(8,128)}, f32[8,256,256]{2,1,0:T(8,128)S(1)}, u32[]{:S(2)}) %copy-start.1) | copy-done | bytes 2097176
  28.7 10.9 %all-to-all-done = f32[256,1,384]{2,1,0:T(1,128)S(1)} async-done(((f32[256,1,384]{2,1,0:T(1,128)}), f32[256,1,384]{2,1,0:T(1,128)S(1)}, u32[]{:S(2)}, u32[]{:S(2)}) %all-to-all-start) | async-done | bytes 393248 | tf_op jit(solution)/shard_map/all_to_all | solution.py:730
  39.6 0.0 copy-start.2
  39.6 3.0 %columns.1 = f32[768,128]{1,0:T(8,128)S(1)} custom-call(f32[768,128]{1,0:T(8,128)S(1)} %bitcast.8, f32[1048,128]{1,0:T(8,128)S(1)} %get-tuple-element.12.numbers, bf16[2048,128]{1,0:T(8,128)(2,1)S(1)} %get-tuple-element.13.terms_in), custom_call_target="tpu_custom_call" | custom-call | tf_op jit(solution)/shard_map/columns/pallas_call | solution.py:693
  42.6 23.2 %all_to_all.10 = f32[256,1,384]{2,1,0:T(1,128)S(1)} all-to-all(f32[256,1,384]{2,1,0:T(1,128)S(1)} %bitcast.10), channel_id=1, replica_groups=mesh['mode'=8,'blk'=32] {'blk','mode'}, dimensions={0} | all-to-all | bytes 786432 | tf_op jit(solution)/shard_map/all_to_all | solution.py:730
  65.8 0.0 copy-done
  65.8 0.0 copy-done.7
  65.8 0.0 copy-done.2
  65.8 3.4 %backward.1 = f32[32,16,1024]{2,1,0:T(8,128)} custom-call(s32[1]{0:T(128)S(6)} %copy.14.levels, f32[768,128]{1,0:T(8,128)S(1)} %bitcast.9, f32[8,256,256]{2,1,0:T(8,128)S(1)} %copy-done.2, bf16[16,256,256]{2,1,0:T(8,128)(2,1)S(1)} %copy-done, f32[1,1024]{1,0:T(1,128)S(1)} %copy-done.7), custom_call_target="tpu_custom_call" | custom-call | tf_op jit(solution)/shard_map/backward/pallas_call | solution.py:711
Async XLA Ops:
  6.8 32.8 %all-to-all-start = ((f32[256,1,384]{2,1,0:T(1,128)}), f32[256,1,384]{2,1,0:T(1,128)S(1)}, u32[]{:S(2)}, u32[]{:S(2)}) async-start(f32[256,1,384]{2,1,0:T(1,128)} %bitcast.12), calls=%async_computation | async-start | bytes 786432 | tf_op jit(solution)/shard_map/all_to_all | solution.py:730
  22.5 1.6 %copy-start.3 = (f32[8,256,256]{2,1,0:T(8,128)S(1)}, f32[8,256,256]{2,1,0:T(8,128)}, u32[]{:S(2)}) copy-start(f32[8,256,256]{2,1,0:T(8,128)} %get-tuple-element.11.w_in) | copy-start | bytes 6291460
  24.1 1.0 %copy-start.4 = (f32[776,128]{1,0:T(8,128)S(1)}, f32[776,128]{1,0:T(8,128)}, u32[]{:S(2)}) copy-start(f32[776,128]{1,0:T(8,128)} %constant.24.clone.constants_in) | copy-start | bytes 1191940
  25.1 0.9 %copy-start.5 = (bf16[4,128,128]{2,1,0:T(8,128)(2,1)S(1)}, bf16[4,128,128]{2,1,0:T(8,128)(2,1)}, u32[]{:S(2)}) copy-start(bf16[4,128,128]{2,1,0:T(8,128)(2,1)} %constant.25.clone.zbasis) | copy-start | bytes 393220
  26.0 0.9 %copy-start.6 = (f32[256,1,128]{2,1,0:T(1,128)S(1)}, f32[256,1,128]{2,1,0:T(1,128)}, u32[]{:S(2)}) copy-start(f32[256,1,128]{2,1,0:T(1,128)} %constant.23.clone.k_own) | copy-start | bytes 393220
  26.9 38.9 %copy-start = (bf16[16,256,256]{2,1,0:T(8,128)(2,1)S(1)}, bf16[16,256,256]{2,1,0:T(8,128)(2,1)}, u32[]{:S(2)}) copy-start(bf16[16,256,256]{2,1,0:T(8,128)(2,1)} %constant.21.clone.tables_in.tables) | copy-start | bytes 6291460
  26.9 38.9 %copy-start.7 = (f32[1,1024]{1,0:T(1,128)S(1)}, f32[1,1024]{1,0:T(1,128)}, u32[]{:S(2)}) copy-start(f32[1,1024]{1,0:T(1,128)} %constant.22.clone.kq) | copy-start | bytes 12292
  27.4 1.3 %copy-start.1 = (f32[8,256,256]{2,1,0:T(8,128)}, f32[8,256,256]{2,1,0:T(8,128)S(1)}, u32[]{:S(2)}) copy-start(f32[8,256,256]{2,1,0:T(8,128)S(1)} %get-tuple-element.14.w_in) | copy-start | bytes 6291460
  39.6 26.2 %copy-start.2 = (f32[8,256,256]{2,1,0:T(8,128)S(1)}, f32[8,256,256]{2,1,0:T(8,128)}, u32[]{:S(2)}) copy-start(f32[8,256,256]{2,1,0:T(8,128)} %copy-done.1) | copy-start | bytes 6291460
